TPU v7x, 256 devices: a whole 4x4x8 slice. The times are simulated.
256 devices in a mesh: seq: 4 (over x_hi, core), tok: 64 (over y, z, x_lo).
Axes of the slice: x: 4 (x_hi: 2, x_lo: 2; x = x_hi * 2 + x_lo), y: 4, z: 8, core: 2. Of those that a mesh axis runs over, the one named last changes fastest.
Arguments:
- query_gate: float32 [4, 32768, 128], P('seq', 'tok'), may hold values from -6 to 6
- key_gate: float32 [4, 32768, 128], P('seq', 'tok'), may hold values from -6 to 6
- value_input: float32 [4, 32768, 128], P('seq', 'tok'), may hold values from -6 to 6
- out_grad: float32 [4, 32768, 128], P('seq', 'tok'), may hold values from -6 to 6
- filter_param: float32 [128, 32768], P('tok', 'seq'), may hold values from -6 to 6
Outputs:
- query_grad: float32 [4, 32768, 128], P('seq', 'tok')
- key_grad: float32 [4, 32768, 128], P('seq', 'tok')
- value_grad: float32 [4, 32768, 128], P('seq', 'tok')
- filter_grad: float32 [128, 32768], P('tok', 'seq')
All inputs are finite; a program needn't handle non-finite values.
Results may differ from a plain program's by a relative error of at most 0.00014.
Values sent between devices are 32-bit elements; how exact they have to be, the bound alone decides.
No kernel may reach another device: no remote copies, remote signals or barrier semaphores. Data moves between devices by JAX's collectives and lax.ppermute only.
A program may use at most 128 MiB of HBM per device.

v0:
```python
import jax
import jax.numpy as jnp
import numpy as np
from jax import lax
from jax.experimental import pallas as pl
from jax.experimental.pallas import tpu as pltpu
from jax.sharding import PartitionSpec as P

TOK = 64
SEQ = 4
ROWS = 512
WIDTH = 128
LENGTH = TOK * ROWS
OUTER = 128
INNER = 256
SCALE = LENGTH**-0.5 / LENGTH

f32 = jnp.float32
bf16 = jnp.bfloat16
VMEM = pl.BlockSpec(memory_space=pltpu.VMEM)
SMEM = pl.BlockSpec(memory_space=pltpu.SMEM)


def split_np(table):
    table = table.astype(np.float32)
    high = table.astype(jnp.bfloat16)
    low = (table - high.astype(np.float32)).astype(jnp.bfloat16)
    return high, low


def tables():
    k1 = np.arange(OUTER, dtype=np.float64)[:, None] + 0.25
    j = np.concatenate([np.arange(0, OUTER, 2), np.arange(1, OUTER, 2)]).astype(np.float64)[None, :]
    outer = 2.0 * np.pi * np.mod(k1 * j, OUTER) / OUTER
    w = np.concatenate([np.cos(outer), -np.sin(outer)], axis=0)
    wh, wl = split_np(w)
    w_fwd = np.concatenate([wh, wh, wl], axis=1)
    vh, vl = split_np(w.T)
    w_inv = np.concatenate([vh, vh, vl], axis=1)
    r = np.arange(INNER, dtype=np.float64)[None, :]
    twist = 2.0 * np.pi * k1 * r / LENGTH
    tw = np.stack([np.cos(twist), -np.sin(twist)]).astype(np.float32)
    inner = 2.0 * np.pi * np.mod(r.T * r, INNER) / INNER
    c, s = np.cos(inner), np.sin(inner)
    t = np.block([[c, -s], [s, c]])
    th, tl = split_np(t)
    t_cat = np.concatenate([th, th, tl], axis=0)
    return w_fwd, w_inv, tw, t_cat


def split(value):
    high = value.astype(bf16)
    low = (value - high.astype(f32)).astype(bf16)
    return high, low


def send_kernel(query_ref, key_ref, value_ref, grad_ref, out_ref):
    for q in range(4):
        rows = pl.ds(q * 128, 128)
        gated = key_ref[rows, :] * value_ref[rows, :]
        cgrad = grad_ref[rows, :] * query_ref[rows, :]
        out_ref[pl.ds(q, 128, stride=8), :] = gated.T
        out_ref[pl.ds(4 + q, 128, stride=8), :] = cgrad.T


def spectral_kernel(
    part_ref, recv_ref, f0_ref, f1_ref, f2_ref, f3_ref, wf_ref, wi_ref, tw_ref, t_ref,
    out_ref, g0_ref, g1_ref, g2_ref, g3_ref,
    taps, cat, spec, terms,
):
    for k, f_ref in enumerate((f0_ref, f1_ref, f2_ref, f3_ref)):
        base = part_ref[k] * 16
        for c in range(2):
            for q2 in range(2):
                for h in range(2):
                    taps[c, pl.ds(pl.multiple_of(q2 * 64 + base, 16), 16), pl.ds(h * 128, 128)] = f_ref[
                        pl.ds(4 * q2 + 2 * h + c, 16, stride=8), :
                    ]

    def store_cat(row, left, right):
        lh, ll = split(left)
        rh, rl = split(right)
        rows = pl.ds(row * OUTER, OUTER)
        cat[rows, 0:256] = lh
        cat[rows, 256:512] = rh
        cat[rows, 512:768] = ll
        cat[rows, 768:1024] = rl
        cat[rows, 1024:1280] = lh
        cat[rows, 1280:1536] = rh

    for sig in range(3):
        for c in range(2):
            if sig < 2:
                x = jnp.concatenate(
                    [
                        jnp.concatenate(
                            [recv_ref[pl.ds(c * 8 + sig * 4 + 2 * q2 + h, 64, stride=16), :] for h in range(2)],
                            axis=1,
                        )
                        for q2 in range(2)
                    ],
                    axis=0,
                )
            else:
                x = taps[c]
            xh, xl = split(x)
            a = jnp.dot(wf_ref[...], jnp.concatenate([xh, xl, xh], axis=0), preferred_element_type=f32)
            ar, ai = a[:OUTER], a[OUTER:]
            tr, ti = tw_ref[0], tw_ref[1]
            store_cat(2 * sig + c, ar * tr - ai * ti, ar * ti + ai * tr)

    spec[...] = jnp.dot(cat[...], t_ref[...], preferred_element_type=f32)

    for c in range(2):
        def part(sig, im):
            return spec[pl.ds((2 * sig + c) * OUTER, OUTER), pl.ds(im * INNER, INNER)]

        gr, gi = part(0, 0), part(0, 1)
        cr, ci = part(1, 0), part(1, 1)
        hr, hi = part(2, 0), part(2, 1)
        store_cat(c, gr * hi + gi * hr, gr * hr - gi * hi)
        store_cat(2 + c, hr * ci - hi * cr, hr * cr + hi * ci)
        store_cat(4 + c, gr * ci - gi * cr, gr * cr + gi * ci)

    spec[...] = jnp.dot(cat[...], t_ref[...], preferred_element_type=f32)

    for sig in range(3):
        for c in range(2):
            rows = pl.ds((2 * sig + c) * OUTER, OUTER)
            di, dr = spec[rows, 0:INNER], spec[rows, INNER : 2 * INNER]
            tr, ti = tw_ref[0], tw_ref[1]
            e = jnp.concatenate([dr * tr + di * ti, di * tr - dr * ti], axis=0)
            eh, el = split(e)
            y = jnp.dot(wi_ref[...], jnp.concatenate([eh, el, eh], axis=0), preferred_element_type=f32)
            y = y * SCALE
            for q2 in range(2):
                for h in range(2):
                    block = y[q2 * 64 : q2 * 64 + 64, h * 128 : h * 128 + 128]
                    if sig < 2:
                        out_ref[pl.ds(c * 8 + sig * 4 + 2 * q2 + h, 64, stride=16), :] = block
                    else:
                        terms[pl.ds(4 * q2 + 2 * h + c, 64, stride=8), :] = block
    for k, g_ref in enumerate((g0_ref, g1_ref, g2_ref, g3_ref)):
        g_ref[...] = terms[pl.ds(pl.multiple_of(part_ref[k] * 128, 128), 128), :]


def finish_kernel(
    recv_ref, query_ref, key_ref, value_ref, grad_ref, g0_ref, g1_ref, g2_ref, g3_ref,
    qg_ref, kg_ref, vg_ref, fg_ref,
):
    for q in range(4):
        rows = pl.ds(q * 128, 128)
        conv = recv_ref[pl.ds(q, 128, stride=8), :].T
        ggrad = recv_ref[pl.ds(4 + q, 128, stride=8), :].T
        qg_ref[rows, :] = grad_ref[rows, :] * conv
        kg_ref[rows, :] = ggrad * value_ref[rows, :]
        vg_ref[rows, :] = ggrad * key_ref[rows, :]
    fg_ref[...] = (g0_ref[...] + g1_ref[...]) + (g2_ref[...] + g3_ref[...])


def shape(*dims, kind=f32):
    return jax.ShapeDtypeStruct(dims, kind)


def body(query_gate, key_gate, value_input, out_grad, filter_param):
    query, key, value, grad = (a.reshape(ROWS, WIDTH) for a in (query_gate, key_gate, value_input, out_grad))
    me = lax.axis_index("seq")
    parts = jnp.bitwise_xor(me, jnp.arange(SEQ, dtype=jnp.int32)).astype(jnp.int32)

    def swap(block, k):
        return lax.ppermute(block, "seq", [(s, s ^ k) for s in range(SEQ)])

    own = filter_param.reshape(2, 64, 128).transpose(1, 0, 2).reshape(128, 128)
    pieces = [own] + [swap(own, k) for k in (1, 2, 3)]
    sent = pl.pallas_call(
        send_kernel,
        out_shape=shape(TOK * 16, 128),
        in_specs=[VMEM] * 4,
        out_specs=VMEM,
        name="send",
    )(query, key, value, grad)
    recv = lax.all_to_all(sent.reshape(TOK, 16, 128), "tok", split_axis=0, concat_axis=0, tiled=True)
    w_fwd, w_inv, tw, t_cat = tables()
    back, *grads = pl.pallas_call(
        spectral_kernel,
        out_shape=(shape(TOK * 16, 128), *[shape(128, 128)] * 4),
        in_specs=[SMEM] + [VMEM] * 9,
        out_specs=(VMEM,) * 5,
        scratch_shapes=[
            pltpu.VMEM((2, OUTER, INNER), f32),
            pltpu.VMEM((6 * OUTER, 6 * INNER), bf16),
            pltpu.VMEM((6 * OUTER, 2 * INNER), f32),
            pltpu.VMEM((SEQ * 128, 128), f32),
        ],
        name="spectral",
    )(parts, recv.reshape(TOK * 16, 128), *pieces, w_fwd, w_inv, tw, t_cat)
    terms = [grads[0]] + [swap(grads[k], k) for k in (1, 2, 3)]
    home = lax.all_to_all(back.reshape(TOK, 16, 128), "tok", split_axis=0, concat_axis=0, tiled=True)
    qg, kg, vg, fg = pl.pallas_call(
        finish_kernel,
        out_shape=(*[shape(ROWS, WIDTH)] * 3, shape(128, 128)),
        in_specs=[VMEM] * 9,
        out_specs=(VMEM,) * 4,
        name="finish",
    )(home.reshape(TOK * 16, 128), query, key, value, grad, *terms)
    filter_grad = fg.reshape(64, 2, 128).transpose(1, 0, 2).reshape(2, 8192)
    return (qg[None], kg[None], vg[None], filter_grad)


def solution(mesh):
    tokens = P("seq", "tok", None)
    taps = P("tok", "seq")
    return jax.shard_map(
        body,
        mesh=mesh,
        in_specs=(tokens, tokens, tokens, tokens, taps),
        out_specs=(tokens, tokens, tokens, taps),
        check_vma=False,
    )
```

profile of v0, /device:TPU:4, one launch (start us, length us, event | category | flops | bytes accessed | tf_op | source)
XLA Modules:
  0.0 67.2 jit_solution(6523650608695207347)
XLA Ops:
  0.6 0.0 copy-start.2
  0.6 2.2 %send.1 = f32[1024,128]{1,0:T(8,128)} custom-call(f32[512,128]{1,0:T(8,128)} %bitcast.24, f32[512,128]{1,0:T(8,128)} %bitcast.26, f32[512,128]{1,0:T(8,128)} %bitcast.28, f32[512,128]{1,0:T(8,128)} %bitcast.30), custom_call_target="tpu_custom_call" | custom-call | tf_op jit(solution)/shard_map/send/pallas_call | solution.py:175
  2.9 12.7 %all-to-all-start = ((f32[64,16,128]{2,1,0:T(8,128)}), f32[64,16,128]{2,1,0:T(8,128)S(1)}, u32[]{:S(2)}, u32[]{:S(2)}) async-start(f32[64,16,128]{2,1,0:T(8,128)} %bitcast.23), calls=%async_computation | async-start | bytes 1048576 | tf_op jit(solution)/shard_map/all_to_all | solution.py:182
  15.6 0.0 copy-done.2
  15.6 0.1 collective-permute-start.2
  15.7 2.7 %collective-permute-start.1 = (f32[128,128]{1,0:T(8,128)S(1)}, f32[128,128]{1,0:T(8,128)S(1)}, u32[]{:S(2)}, u32[]{:S(2)}) collective-permute-start(f32[128,128]{1,0:T(8,128)S(1)} %bitcast.35), channel_id=1, source_target_pairs={{0,128},{64,192},{128,0},{192,64},{1,129},{65,193},{129,1},{193,65... | collective-permute-start | bytes 196616 | tf_op jit(solution)/shard_map/ppermute | solution.py:171
  18.4 0.7 %collective-permute-start = (f32[128,128]{1,0:T(8,128)S(1)}, f32[128,128]{1,0:T(8,128)S(1)}, u32[]{:S(2)}, u32[]{:S(2)}) collective-permute-start(f32[128,128]{1,0:T(8,128)S(1)} %bitcast.36), channel_id=1, source_target_pairs={{0,64},{64,0},{128,192},{192,128},{1,65},{65,1},{129,193},{193,129... | collective-permute-start | bytes 196616 | tf_op jit(solution)/shard_map/ppermute | solution.py:171
  19.1 0.6 iota_xor_fusion.part_ref
  19.7 3.3 %collective-permute-done.2.f3_ref = f32[128,128]{1,0:T(8,128)S(1)} collective-permute-done((f32[128,128]{1,0:T(8,128)S(1)}, f32[128,128]{1,0:T(8,128)S(1)}, u32[]{:S(2)}, u32[]{:S(2)}) %collective-permute-start.2) | collective-permute-done | bytes 65568 | tf_op jit(solution)/shard_map/ppermute | solution.py:171
  22.9 0.0 copy-start.3
  22.9 1.8 %collective-permute-done.1.f2_ref = f32[128,128]{1,0:T(8,128)S(1)} collective-permute-done((f32[128,128]{1,0:T(8,128)S(1)}, f32[128,128]{1,0:T(8,128)S(1)}, u32[]{:S(2)}, u32[]{:S(2)}) %collective-permute-start.1) | collective-permute-done | bytes 65568 | tf_op jit(solution)/shard_map/ppermute | solution.py:171
  24.7 0.0 copy-start.4
  24.7 0.0 collective-permute-done.f1_ref
  24.8 0.0 copy-start.5
  24.8 8.5 %all-to-all-done = f32[64,16,128]{2,1,0:T(8,128)S(1)} async-done(((f32[64,16,128]{2,1,0:T(8,128)}), f32[64,16,128]{2,1,0:T(8,128)S(1)}, u32[]{:S(2)}, u32[]{:S(2)}) %all-to-all-start) | async-done | bytes 524320 | tf_op jit(solution)/shard_map/all_to_all | solution.py:182
  33.2 0.0 copy-start
  33.2 0.0 copy-done.3
  33.2 0.0 copy-done.4
  33.2 0.0 copy-done.5
  33.2 0.8 %copy-done = f32[64,16,128]{2,1,0:T(8,128)} copy-done((f32[64,16,128]{2,1,0:T(8,128)}, f32[64,16,128]{2,1,0:T(8,128)S(1)}, u32[]{:S(2)}) %copy-start) | copy-done | bytes 524312
  34.0 6.6 %spectral.1 = (f32[1024,128]{1,0:T(8,128)}, f32[128,128]{1,0:T(8,128)}, f32[128,128]{1,0:T(8,128)}, f32[128,128]{1,0:T(8,128)}, f32[128,128]{1,0:T(8,128)}) custom-call(s32[4]{0:T(128)} %iota_xor_fusion.part_ref, f32[1024,128]{1,0:T(8,128)} %bitcast.21, f32[128,128]{1,0:T(8,128)} %bitcast.33, f32[128,128]{1,0:T(8,128)} %copy-done.5, f32[128,128]{1,0:T(8,128)} %copy-done.4, ...), custom_call_target="tpu_custom_call" | custom-call | tf_op jit(solution)/shard_map/spectral/pallas_call | solution.py:184
  40.7 6.0 %all-to-all-start.1 = ((f32[64,16,128]{2,1,0:T(8,128)}), f32[64,16,128]{2,1,0:T(8,128)S(1)}, u32[]{:S(2)}, u32[]{:S(2)}) async-start(f32[64,16,128]{2,1,0:T(8,128)} %bitcast.32), calls=%async_computation.1 | async-start | bytes 1048576 | tf_op jit(solution)/shard_map/all_to_all | solution.py:198
  46.7 0.1 collective-permute-start.3
  46.8 0.9 %collective-permute-start.4 = (f32[128,128]{1,0:T(8,128)}, f32[128,128]{1,0:T(8,128)S(1)}, u32[]{:S(2)}, u32[]{:S(2)}) collective-permute-start(f32[128,128]{1,0:T(8,128)} %get-tuple-element.16), channel_id=1, source_target_pairs={{0,128},{64,192},{128,0},{192,64},{1,129},{65,193},{129,1},{193,65... | collective-permute-start | bytes 196616 | tf_op jit(solution)/shard_map/ppermute | solution.py:171
  47.7 2.5 %collective-permute-start.5 = (f32[128,128]{1,0:T(8,128)}, f32[128,128]{1,0:T(8,128)S(1)}, u32[]{:S(2)}, u32[]{:S(2)}) collective-permute-start(f32[128,128]{1,0:T(8,128)} %get-tuple-element.17), channel_id=1, source_target_pairs={{0,192},{64,128},{128,64},{192,0},{1,193},{65,129},{129,65},{193,1... | collective-permute-start | bytes 196616 | tf_op jit(solution)/shard_map/ppermute | solution.py:171
  50.2 0.0 collective-permute-done.3.g1_ref
  50.2 0.0 copy-start.6
  50.2 4.6 %collective-permute-done.4.g2_ref = f32[128,128]{1,0:T(8,128)S(1)} collective-permute-done((f32[128,128]{1,0:T(8,128)}, f32[128,128]{1,0:T(8,128)S(1)}, u32[]{:S(2)}, u32[]{:S(2)}) %collective-permute-start.4) | collective-permute-done | bytes 65568 | tf_op jit(solution)/shard_map/ppermute | solution.py:171
  54.8 0.0 copy-start.7
  54.8 0.5 collective-permute-done.5.g3_ref
  55.3 0.0 copy-start.8
  55.3 8.6 %all-to-all-done.1 = f32[64,16,128]{2,1,0:T(8,128)S(1)} async-done(((f32[64,16,128]{2,1,0:T(8,128)}), f32[64,16,128]{2,1,0:T(8,128)S(1)}, u32[]{:S(2)}, u32[]{:S(2)}) %all-to-all-start.1) | async-done | bytes 524320 | tf_op jit(solution)/shard_map/all_to_all | solution.py:198
  63.9 0.0 copy-start.1
  63.9 0.0 copy-done.6
  63.9 0.0 copy-done.7
  63.9 0.0 copy-done.8
  64.0 0.8 %copy-done.1 = f32[64,16,128]{2,1,0:T(8,128)} copy-done((f32[64,16,128]{2,1,0:T(8,128)}, f32[64,16,128]{2,1,0:T(8,128)S(1)}, u32[]{:S(2)}) %copy-start.1) | copy-done | bytes 524312
  64.7 2.5 %finish.1 = (f32[512,128]{1,0:T(8,128)}, f32[512,128]{1,0:T(8,128)}, f32[512,128]{1,0:T(8,128)}, f32[128,128]{1,0:T(8,128)}) custom-call(f32[1024,128]{1,0:T(8,128)} %bitcast.22, f32[512,128]{1,0:T(8,128)} %bitcast.25, f32[512,128]{1,0:T(8,128)} %bitcast.27, f32[512,128]{1,0:T(8,128)} %bitcast.29, f32[512,128]{1,0:T(8,128)} %bitcast.31, ...), custom_call_target="tpu_custom_call" | custom-call | tf_op jit(solution)/shard_map/finish/pallas_call | solution.py:199
Async XLA Ops:
  0.6 15.0 %copy-start.2 = (f32[2,8192]{1,0:T(2,128)S(1)}, f32[2,8192]{1,0:T(2,128)}, u32[]{:S(2)}) copy-start(f32[2,8192]{1,0:T(2,128)} %param.13) | copy-start | bytes 196612
  2.9 30.4 %all-to-all-start = ((f32[64,16,128]{2,1,0:T(8,128)}), f32[64,16,128]{2,1,0:T(8,128)S(1)}, u32[]{:S(2)}, u32[]{:S(2)}) async-start(f32[64,16,128]{2,1,0:T(8,128)} %bitcast.23), calls=%async_computation | async-start | bytes 1048576 | tf_op jit(solution)/shard_map/all_to_all | solution.py:182
  15.6 7.3 %collective-permute-start.2 = (f32[128,128]{1,0:T(8,128)S(1)}, f32[128,128]{1,0:T(8,128)S(1)}, u32[]{:S(2)}, u32[]{:S(2)}) collective-permute-start(f32[128,128]{1,0:T(8,128)S(1)} %bitcast.34), channel_id=1, source_target_pairs={{0,192},{64,128},{128,64},{192,0},{1,193},{65,129},{129,65},{193,1... | collective-permute-start | bytes 196616 | tf_op jit(solution)/shard_map/ppermute | solution.py:171
  15.7 9.0 %collective-permute-start.1 = (f32[128,128]{1,0:T(8,128)S(1)}, f32[128,128]{1,0:T(8,128)S(1)}, u32[]{:S(2)}, u32[]{:S(2)}) collective-permute-start(f32[128,128]{1,0:T(8,128)S(1)} %bitcast.35), channel_id=1, source_target_pairs={{0,128},{64,192},{128,0},{192,64},{1,129},{65,193},{129,1},{193,65... | collective-permute-start | bytes 196616 | tf_op jit(solution)/shard_map/ppermute | solution.py:171
  18.4 6.4 %collective-permute-start = (f32[128,128]{1,0:T(8,128)S(1)}, f32[128,128]{1,0:T(8,128)S(1)}, u32[]{:S(2)}, u32[]{:S(2)}) collective-permute-start(f32[128,128]{1,0:T(8,128)S(1)} %bitcast.36), channel_id=1, source_target_pairs={{0,64},{64,0},{128,192},{192,128},{1,65},{65,1},{129,193},{193,129... | collective-permute-start | bytes 196616 | tf_op jit(solution)/shard_map/ppermute | solution.py:171
  22.9 10.3 %copy-start.3 = (f32[128,128]{1,0:T(8,128)}, f32[128,128]{1,0:T(8,128)S(1)}, u32[]{:S(2)}) copy-start(f32[128,128]{1,0:T(8,128)S(1)} %collective-permute-done.2.f3_ref) | copy-start | bytes 196612
  24.7 8.5 %copy-start.4 = (f32[128,128]{1,0:T(8,128)}, f32[128,128]{1,0:T(8,128)S(1)}, u32[]{:S(2)}) copy-start(f32[128,128]{1,0:T(8,128)S(1)} %collective-permute-done.1.f2_ref) | copy-start | bytes 196612
  24.8 8.5 %copy-start.5 = (f32[128,128]{1,0:T(8,128)}, f32[128,128]{1,0:T(8,128)S(1)}, u32[]{:S(2)}) copy-start(f32[128,128]{1,0:T(8,128)S(1)} %collective-permute-done.f1_ref) | copy-start | bytes 196612
  33.2 0.8 %copy-start = (f32[64,16,128]{2,1,0:T(8,128)}, f32[64,16,128]{2,1,0:T(8,128)S(1)}, u32[]{:S(2)}) copy-start(f32[64,16,128]{2,1,0:T(8,128)S(1)} %all-to-all-done) | copy-start | bytes 1572868
  40.7 23.3 %all-to-all-start.1 = ((f32[64,16,128]{2,1,0:T(8,128)}), f32[64,16,128]{2,1,0:T(8,128)S(1)}, u32[]{:S(2)}, u32[]{:S(2)}) async-start(f32[64,16,128]{2,1,0:T(8,128)} %bitcast.32), calls=%async_computation.1 | async-start | bytes 1048576 | tf_op jit(solution)/shard_map/all_to_all | solution.py:198
  46.7 3.5 %collective-permute-start.3 = (f32[128,128]{1,0:T(8,128)}, f32[128,128]{1,0:T(8,128)S(1)}, u32[]{:S(2)}, u32[]{:S(2)}) collective-permute-start(f32[128,128]{1,0:T(8,128)} %get-tuple-element.15), channel_id=1, source_target_pairs={{0,64},{64,0},{128,192},{192,128},{1,65},{65,1},{129,193},{193,129... | collective-permute-start | bytes 196616 | tf_op jit(solution)/shard_map/ppermute | solution.py:171
  46.8 8.0 %collective-permute-start.4 = (f32[128,128]{1,0:T(8,128)}, f32[128,128]{1,0:T(8,128)S(1)}, u32[]{:S(2)}, u32[]{:S(2)}) collective-permute-start(f32[128,128]{1,0:T(8,128)} %get-tuple-element.16), channel_id=1, source_target_pairs={{0,128},{64,192},{128,0},{192,64},{1,129},{65,193},{129,1},{193,65... | collective-permute-start | bytes 196616 | tf_op jit(solution)/shard_map/ppermute | solution.py:171
  47.7 7.6 %collective-permute-start.5 = (f32[128,128]{1,0:T(8,128)}, f32[128,128]{1,0:T(8,128)S(1)}, u32[]{:S(2)}, u32[]{:S(2)}) collective-permute-start(f32[128,128]{1,0:T(8,128)} %get-tuple-element.17), channel_id=1, source_target_pairs={{0,192},{64,128},{128,64},{192,0},{1,193},{65,129},{129,65},{193,1... | collective-permute-start | bytes 196616 | tf_op jit(solution)/shard_map/ppermute | solution.py:171
  50.2 13.8 %copy-start.6 = (f32[128,128]{1,0:T(8,128)}, f32[128,128]{1,0:T(8,128)S(1)}, u32[]{:S(2)}) copy-start(f32[128,128]{1,0:T(8,128)S(1)} %collective-permute-done.3.g1_ref) | copy-start | bytes 196612
  54.8 9.2 %copy-start.7 = (f32[128,128]{1,0:T(8,128)}, f32[128,128]{1,0:T(8,128)S(1)}, u32[]{:S(2)}) copy-start(f32[128,128]{1,0:T(8,128)S(1)} %collective-permute-done.4.g2_ref) | copy-start | bytes 196612
  55.3 8.6 %copy-start.8 = (f32[128,128]{1,0:T(8,128)}, f32[128,128]{1,0:T(8,128)S(1)}, u32[]{:S(2)}) copy-start(f32[128,128]{1,0:T(8,128)S(1)} %collective-permute-done.5.g3_ref) | copy-start | bytes 196612
  63.9 0.8 %copy-start.1 = (f32[64,16,128]{2,1,0:T(8,128)}, f32[64,16,128]{2,1,0:T(8,128)S(1)}, u32[]{:S(2)}) copy-start(f32[64,16,128]{2,1,0:T(8,128)S(1)} %all-to-all-done.1) | copy-start | bytes 1572868
where the time goes:
time: 67.5 us; the launch traced here: 67.2 us
  waiting for transfers between devices  27.3 us (40%)
  starting transfers between devices  25.7 us (38%)
  Pallas kernels  11.3 us (17%)
  local copies, waits for them, and re-layouts  1.59 us (2%)
  between operations  0.7 us (1%)
    all_to_all x1, starting transfers between devices, body(): lax.all_to_all(sent.reshape(TOK, 16, 128), 'tok', split_axis=0, concat_ax...  12.7 us
    ppermute x6, waiting for transfers between devices, swap(): return lax.ppermute(block, 'seq', [(s, s ^ k) for s in range(SEQ)])  10.2 us
    all_to_all x1, waiting for transfers between devices, body(): lax.all_to_all(back.reshape(TOK, 16, 128), 'tok', split_axis=0, concat_ax...  8.63 us
    all_to_all x1, waiting for transfers between devices, body(): lax.all_to_all(sent.reshape(TOK, 16, 128), 'tok', split_axis=0, concat_ax...  8.47 us
    ppermute x6, starting transfers between devices, swap(): return lax.ppermute(block, 'seq', [(s, s ^ k) for s in range(SEQ)])  6.89 us
    pallas_call x1, Pallas kernels, body(): pl.pallas_call(spectral_kernel, out_shape=(shape(TOK * 16, 128), *[shape(...  6.64 us
    all_to_all x1, starting transfers between devices, body(): lax.all_to_all(back.reshape(TOK, 16, 128), 'tok', split_axis=0, concat_ax...  6.04 us
    pallas_call x1, Pallas kernels, body(): pl.pallas_call(finish_kernel, out_shape=(*[shape(ROWS, WIDTH)] * 3, shape...  2.47 us
  transfers between devices with their start and end apart: 8, of which 6 were waited for; matrix products, arithmetic and copies ran while one was open for 1% of the time, Pallas kernels for 0%

commit v1 on v0

v1 whole, which is shorter than its diff:
```python
import jax
import jax.numpy as jnp
import numpy as np
from jax import lax
from jax.experimental import pallas as pl
from jax.experimental.pallas import tpu as pltpu
from jax.sharding import PartitionSpec as P

TOK = 64
SEQ = 4
ROWS = 512
WIDTH = 128
LENGTH = TOK * ROWS
OUTER = 128
INNER = 256
HALF = INNER // 2
SCALE = LENGTH**-0.5 / LENGTH

PIECE = (0, 2, 1, 3)

f32 = jnp.float32
bf16 = jnp.bfloat16
VMEM = pl.BlockSpec(memory_space=pltpu.VMEM)
HBM = pl.BlockSpec(memory_space=pltpu.HBM)
SMEM = pl.BlockSpec(memory_space=pltpu.SMEM)


def split_np(table):
    table = table.astype(np.float32)
    high = table.astype(jnp.bfloat16)
    low = (table - high.astype(np.float32)).astype(jnp.bfloat16)
    return high, low


def stack_np(real, imag, left):
    high, low = split_np(np.block([[real, imag], [-imag, real]]))
    return np.concatenate([high, high, low], axis=1 if left else 0)


def tables():
    k1 = np.arange(OUTER, dtype=np.float64)[:, None] + 0.25
    j = np.concatenate([np.arange(0, OUTER, 2), np.arange(1, OUTER, 2)]).astype(np.float64)[None, :]
    outer = 2.0 * np.pi * np.mod(k1 * j, OUTER) / OUTER
    w = np.concatenate([np.cos(outer), -np.sin(outer)], axis=0)
    wh, wl = split_np(w)
    w_fwd = np.concatenate([wh, wh, wl], axis=1)
    vh, vl = split_np(w.T)
    w_inv = np.concatenate([vh, vh, vl], axis=1)
    r = np.arange(INNER, dtype=np.float64)[None, :]
    twist = 2.0 * np.pi * k1 * r / LENGTH
    tw = np.stack([np.cos(twist), -np.sin(twist)]).astype(np.float32)
    l = np.arange(HALF, dtype=np.float64)[:, None]
    m = np.arange(HALF, dtype=np.float64)[None, :]
    even = 2.0 * np.pi * np.mod(l * 2 * m, INNER) / INNER
    odd = 2.0 * np.pi * np.mod(l * (2 * m + 1), INNER) / INNER
    t_even = stack_np(np.cos(even), -np.sin(even), False)
    t_odd = stack_np(np.cos(odd), -np.sin(odd), False)
    t_back = stack_np(np.cos(odd.T), -np.sin(odd.T), False)
    return w_fwd, w_inv, tw, t_even, t_odd, t_back


def split(value):
    high = value.astype(bf16)
    low = (value - high.astype(f32)).astype(bf16)
    return high, low


def send_kernel(query_hbm, key_hbm, value_hbm, grad_hbm, out_hbm, query, key, value, grad, tiles, sem, out_sem):
    pairs = ((query_hbm, query), (key_hbm, key), (value_hbm, value), (grad_hbm, grad))
    copies, sends = [], []
    for q in range(4):
        rows = pl.ds(q * 128, 128)
        copies.append([pltpu.make_async_copy(a.at[rows], b.at[rows], sem.at[q, i]) for i, (a, b) in enumerate(pairs)])
        for copy in copies[q]:
            copy.start()
    for q in range(4):
        rows = pl.ds(q * 128, 128)
        for copy in copies[q]:
            copy.wait()
        tiles[q] = (key[rows, :] * value[rows, :]).T
        tiles[4 + q] = (grad[rows, :] * query[rows, :]).T
        for i in (q, 4 + q):
            sends.append(pltpu.make_async_copy(tiles.at[i], out_hbm.at[:, i, :], out_sem.at[i]))
            sends[-1].start()
    for send in sends:
        send.wait()


def store_cat(cat, row, left, right):
    lh, ll = split(left)
    rh, rl = split(right)
    rows = pl.ds(row * OUTER, OUTER)
    cat[rows, 0:128] = lh
    cat[rows, 128:256] = rh
    cat[rows, 256:384] = ll
    cat[rows, 384:512] = rl
    cat[rows, 512:640] = lh
    cat[rows, 640:768] = rh


def forward_outer(x, row, wf_ref, tw_ref, cat_e, cat_o):
    xh, xl = split(x)
    a = jnp.dot(wf_ref[...], jnp.concatenate([xh, xl, xh], axis=0), preferred_element_type=f32)
    ar, ai = a[:OUTER], a[OUTER:]
    tr, ti = tw_ref[0], tw_ref[1]
    br, bi = ar * tr - ai * ti, ar * ti + ai * tr
    store_cat(cat_e, row, br[:, :HALF] + br[:, HALF:], bi[:, :HALF] + bi[:, HALF:])
    store_cat(cat_o, row, br[:, :HALF] - br[:, HALF:], bi[:, :HALF] - bi[:, HALF:])


def inverse_outer(spec_e, spec_o, row, wi_ref, tw_ref):
    rows = pl.ds(row * OUTER, OUTER)
    ei, er = spec_e[rows, 0:HALF], spec_e[rows, HALF : 2 * HALF]
    oi, orr = spec_o[rows, 0:HALF], spec_o[rows, HALF : 2 * HALF]
    dr = jnp.concatenate([er + orr, er - orr], axis=1)
    di = jnp.concatenate([ei + oi, ei - oi], axis=1)
    tr, ti = tw_ref[0], tw_ref[1]
    e = jnp.concatenate([dr * tr + di * ti, di * tr - dr * ti], axis=0)
    eh, el = split(e)
    y = jnp.dot(wi_ref[...], jnp.concatenate([eh, el, eh], axis=0), preferred_element_type=f32)
    return y * SCALE


def matmul(cat, table):
    return jnp.dot(cat[...], table[...], preferred_element_type=f32)


def taps_kernel(
    part_ref, near_ref, far_ref, wf_ref, tw_ref, te_ref, to_ref, out_hbm, taps, cat_e, cat_o, spec, sem
):
    for k in range(SEQ):
        f_ref, first = (near_ref if k < 2 else far_ref), (k % 2) * 128
        base = part_ref[PIECE[k]] * 16
        for c in range(2):
            for q2 in range(2):
                for h in range(2):
                    taps[c, pl.ds(pl.multiple_of(q2 * 64 + base, 16), 16), pl.ds(h * 128, 128)] = f_ref[
                        pl.ds(first + 4 * q2 + 2 * h + c, 16, stride=8), :
                    ]
    for c in range(2):
        forward_outer(taps[c], c, wf_ref, tw_ref, cat_e, cat_o)
    copies = []
    for p, (cat, t_ref) in enumerate(((cat_e, te_ref), (cat_o, to_ref))):
        spec[p] = matmul(cat, t_ref)
        copies.append(pltpu.make_async_copy(spec.at[p], out_hbm.at[p], sem.at[p]))
        copies[p].start()
    for copy in copies:
        copy.wait()


def spectral_kernel(
    recv_ref, taps_ref, wf_ref, wi_ref, tw_ref, te_ref, to_ref, tb_ref,
    out_hbm, cross_hbm,
    cat_e, cat_o, spec_e, spec_o, cross, tiles, sem, out_sem,
):
    for sig in range(2):
        for c in range(2):
            x = jnp.concatenate(
                [
                    jnp.concatenate(
                        [recv_ref[pl.ds(c * 8 + sig * 4 + 2 * q2 + h, 64, stride=16), :] for h in range(2)],
                        axis=1,
                    )
                    for q2 in range(2)
                ],
                axis=0,
            )
            forward_outer(x, 2 * sig + c, wf_ref, tw_ref, cat_e, cat_o)

    spec_e[...] = matmul(cat_e, te_ref)
    spec_o[...] = matmul(cat_o, to_ref)

    for p, (cat, spec) in enumerate(((cat_e, spec_e), (cat_o, spec_o))):
        for c in range(2):
            def part(ref, row, im):
                return ref[pl.ds(row * OUTER, OUTER), pl.ds(im * HALF, HALF)]

            gr, gi = part(spec, c, 0), part(spec, c, 1)
            cr, ci = part(spec, 2 + c, 0), part(spec, 2 + c, 1)
            hr, hi = part(taps_ref.at[p], c, 0), part(taps_ref.at[p], c, 1)
            store_cat(cat, c, gr * hi + gi * hr, gr * hr - gi * hi)
            store_cat(cat, 2 + c, hr * ci - hi * cr, hr * cr + hi * ci)
            cross[p, pl.ds(c * OUTER, OUTER), 0:HALF] = gr * ci - gi * cr
            cross[p, pl.ds(c * OUTER, OUTER), HALF : 2 * HALF] = gr * cr + gi * ci

    sends = [pltpu.make_async_copy(cross, cross_hbm, sem)]
    sends[0].start()
    spec_e[...] = matmul(cat_e, te_ref)
    spec_o[...] = matmul(cat_o, tb_ref)

    for sig in range(2):
        for c in range(2):
            y = inverse_outer(spec_e, spec_o, 2 * sig + c, wi_ref, tw_ref)
            for q2 in range(2):
                for h in range(2):
                    i = c * 8 + sig * 4 + 2 * q2 + h
                    tiles[i] = y[q2 * 64 : q2 * 64 + 64, h * 128 : h * 128 + 128]
                    sends.append(pltpu.make_async_copy(tiles.at[i], out_hbm.at[:, i, :], out_sem.at[i]))
                    sends[-1].start()
    for send in sends:
        send.wait()


def terms_kernel(
    part_ref, cross_ref, wi_ref, tw_ref, te_ref, tb_ref, own_ref, give_ref, cat_e, cat_o, spec_e, spec_o, terms
):
    for p, cat in enumerate((cat_e, cat_o)):
        for c in range(2):
            rows = pl.ds(c * OUTER, OUTER)
            store_cat(cat, c, cross_ref[p, rows, 0:HALF], cross_ref[p, rows, HALF : 2 * HALF])
    spec_e[...] = matmul(cat_e, te_ref)
    spec_o[...] = matmul(cat_o, tb_ref)
    for c in range(2):
        y = inverse_outer(spec_e, spec_o, c, wi_ref, tw_ref)
        for q2 in range(2):
            for h in range(2):
                terms[pl.ds(4 * q2 + 2 * h + c, 64, stride=8), :] = y[
                    q2 * 64 : q2 * 64 + 64, h * 128 : h * 128 + 128
                ]
    for k in range(SEQ):
        ref, first = (own_ref if k < 2 else give_ref), (k % 2) * 128
        ref[first : first + 128, :] = terms[
            pl.ds(pl.multiple_of(part_ref[PIECE[k]] * 128, 128), 128), :
        ]


def finish_kernel(
    recv_ref, query_ref, key_ref, value_ref, grad_ref, own_ref, far_ref,
    qg_hbm, kg_hbm, vg_hbm, fg_hbm,
    qg, kg, vg, fg, sem,
):
    fg[...] = own_ref[...] + far_ref[...]
    copies = [pltpu.make_async_copy(fg, fg_hbm, sem.at[12])]
    copies[0].start()
    for q in range(4):
        rows = pl.ds(q * 128, 128)
        conv = recv_ref[pl.ds(q, 128, stride=8), :].T
        ggrad = recv_ref[pl.ds(4 + q, 128, stride=8), :].T
        qg[rows, :] = grad_ref[rows, :] * conv
        kg[rows, :] = ggrad * value_ref[rows, :]
        vg[rows, :] = ggrad * key_ref[rows, :]
        for i, (a, b) in enumerate(((qg, qg_hbm), (kg, kg_hbm), (vg, vg_hbm))):
            copy = pltpu.make_async_copy(a.at[rows], b.at[rows], sem.at[3 * q + i])
            copy.start()
            copies.append(copy)
    for copy in copies:
        copy.wait()


def shape(*dims, kind=f32):
    return jax.ShapeDtypeStruct(dims, kind)


def room(mib):
    return pltpu.CompilerParams(vmem_limit_bytes=mib * 2**20)


def cost(units):
    return pl.CostEstimate(flops=units * 800_000_000, bytes_accessed=units * 1_000_000, transcendentals=0)


def body(query_gate, key_gate, value_input, out_grad, filter_param):
    query, key, value, grad = (a.reshape(ROWS, WIDTH) for a in (query_gate, key_gate, value_input, out_grad))
    me = lax.axis_index("seq")
    parts = jnp.bitwise_xor(me, jnp.arange(SEQ, dtype=jnp.int32)).astype(jnp.int32)

    def swap(block, k):
        return lax.ppermute(block, "seq", [(s, s ^ k) for s in range(SEQ)])

    own = filter_param.reshape(2, 64, 128).transpose(1, 0, 2).reshape(128, 128)
    near = jnp.concatenate([own, swap(own, 2)], axis=0)
    far = swap(near, 1)
    w_fwd, w_inv, tw, t_even, t_odd, t_back = tables()
    sent = pl.pallas_call(
        send_kernel,
        out_shape=shape(TOK * 2, 8, 128),
        in_specs=[HBM] * 4,
        out_specs=HBM,
        scratch_shapes=[pltpu.VMEM((ROWS, WIDTH), f32)] * 4
        + [pltpu.VMEM((8, 128, 128), f32), pltpu.SemaphoreType.DMA((4, 4)), pltpu.SemaphoreType.DMA((8,))],
        compiler_params=room(60),
        name="send",
    )(query, key, value, grad)
    recv = lax.all_to_all(sent.reshape(TOK, 16, 128), "tok", split_axis=0, concat_axis=0, tiled=True)
    taps = pl.pallas_call(
        taps_kernel,
        out_shape=shape(2, 2 * OUTER, INNER),
        in_specs=[SMEM] + [VMEM] * 6,
        out_specs=HBM,
        scratch_shapes=[pltpu.VMEM((2, OUTER, INNER), f32)]
        + [pltpu.VMEM((2 * OUTER, 3 * INNER), bf16)] * 2
        + [pltpu.VMEM((2, 2 * OUTER, INNER), f32), pltpu.SemaphoreType.DMA((2,))],
        compiler_params=room(8),
        cost_estimate=cost(1),
        name="taps",
    )(parts, near, far, w_fwd, tw, t_even, t_odd)
    back, cross = pl.pallas_call(
        spectral_kernel,
        out_shape=(shape(TOK, 16, 128), pltpu.HBM((2, 2 * OUTER, INNER), f32)),
        in_specs=[VMEM] * 8,
        out_specs=(HBM, HBM),
        scratch_shapes=[pltpu.VMEM((4 * OUTER, 3 * INNER), bf16)] * 2
        + [pltpu.VMEM((4 * OUTER, INNER), f32)] * 2
        + [pltpu.VMEM((2, 2 * OUTER, INNER), f32)]
        + [pltpu.VMEM((16, TOK, 128), f32), pltpu.SemaphoreType.DMA, pltpu.SemaphoreType.DMA((16,))],
        compiler_params=room(8),
        cost_estimate=cost(4),
        name="spectral",
    )(recv.reshape(TOK * 16, 128), taps, w_fwd, w_inv, tw, t_even, t_odd, t_back)
    home = lax.all_to_all(back.reshape(TOK, 16, 128), "tok", split_axis=0, concat_axis=0, tiled=True)
    kept, given = pl.pallas_call(
        terms_kernel,
        out_shape=(shape(256, 128),) * 2,
        in_specs=[SMEM] + [VMEM] * 5,
        out_specs=(VMEM,) * 2,
        scratch_shapes=[pltpu.VMEM((2 * OUTER, 3 * INNER), bf16)] * 2
        + [pltpu.VMEM((2 * OUTER, INNER), f32)] * 2
        + [pltpu.VMEM((SEQ * 128, 128), f32)],
        compiler_params=room(8),
        cost_estimate=cost(1),
        name="terms",
    )(parts, cross, w_inv, tw, t_even, t_back)
    paired = kept + swap(given, 1)
    terms = (paired[:128], swap(paired[128:], 2))
    qg, kg, vg, fg = pl.pallas_call(
        finish_kernel,
        out_shape=(*[shape(ROWS, WIDTH)] * 3, shape(128, 128)),
        in_specs=[VMEM] * 7,
        out_specs=(HBM,) * 4,
        scratch_shapes=[pltpu.VMEM((ROWS, WIDTH), f32)] * 3
        + [pltpu.VMEM((128, 128), f32), pltpu.SemaphoreType.DMA((13,))],
        compiler_params=room(8),
        name="finish",
    )(home.reshape(TOK * 16, 128), query, key, value, grad, *terms)
    filter_grad = fg.reshape(64, 2, 128).transpose(1, 0, 2).reshape(2, 8192)
    return (qg[None], kg[None], vg[None], filter_grad)


def solution(mesh):
    tokens = P("seq", "tok", None)
    taps = P("tok", "seq")
    return jax.shard_map(
        body,
        mesh=mesh,
        in_specs=(tokens, tokens, tokens, tokens, taps),
        out_specs=(tokens, tokens, tokens, taps),
        check_vma=False,
    )
```

time: 67.5 us -> 61.6 us (0.913)
  starting transfers between devices: 25.7 us -> 21 us
  waiting for transfers between devices: 27.3 us -> 29.7 us
  Pallas kernels: 11.3 us -> 9.6 us
  local copies, waits for them, and re-layouts: 1.59 us -> 0.08 us
    ppermute x6 -> x4, starting transfers between devices: 6.89 us -> 1.95 us  [swap(): return lax.ppermute(block, 'seq', [(s, s ^ k) for s in range(SEQ)])]
    ppermute x6 -> x4, waiting for transfers between devices: 10.2 us -> 13.3 us  [swap(): return lax.ppermute(block, 'seq', [(s, s ^ k) for s in range(SEQ)])]
    unnamed x18 -> x24, local copies, waits for them, and re-layouts: 1.59 us -> 0.07 us
    pallas_call x1, Pallas kernels: 2.47 us -> 1.08 us  [body(): pl.pallas_call(finish_kernel, out_shape=(*[shape(ROWS, WIDTH)] * 3, shape...]
    pallas_call x2 -> x4, Pallas kernels: 8.86 us -> 8.51 us  [the longest x1 3.27 us: body(): pl.pallas_call(spectral_kernel, out_shape=(shape(TOK, 16, 128), pltpu.HBM...]
  transfers between devices with their start and end apart: 8 -> 6, of which waited for: 6 -> 6; matrix products, arithmetic and copies ran while one was open for 1% -> 0% of each run, Pallas kernels for 0% -> 5%
where the time goes in v1:
time: 61.6 us; the launch traced here: 61.3 us
  waiting for transfers between devices  29.7 us (48%)
  starting transfers between devices  21 us (34%)
  Pallas kernels  9.6 us (16%)
  between operations  0.84 us (1%)
    ppermute x4, waiting for transfers between devices, swap(): return lax.ppermute(block, 'seq', [(s, s ^ k) for s in range(SEQ)])  13.3 us
    all_to_all x1, starting transfers between devices, body(): lax.all_to_all(sent.reshape(TOK, 16, 128), 'tok', split_axis=0, concat_ax...  12.9 us
    all_to_all x1, waiting for transfers between devices, body(): lax.all_to_all(sent.reshape(TOK, 16, 128), 'tok', split_axis=0, concat_ax...  8.22 us
    all_to_all x1, waiting for transfers between devices, body(): lax.all_to_all(back.reshape(TOK, 16, 128), 'tok', split_axis=0, concat_ax...  8.16 us
    all_to_all x1, starting transfers between devices, body(): lax.all_to_all(back.reshape(TOK, 16, 128), 'tok', split_axis=0, concat_ax...  6.18 us
    pallas_call x1, Pallas kernels, body(): pl.pallas_call(spectral_kernel, out_shape=(shape(TOK, 16, 128), pltpu.HBM...  3.27 us
    pallas_call x1, Pallas kernels, body(): pl.pallas_call(send_kernel, out_shape=shape(TOK * 2, 8, 128), in_specs=[H...  2.28 us
    ppermute x4, starting transfers between devices, swap(): return lax.ppermute(block, 'seq', [(s, s ^ k) for s in range(SEQ)])  1.95 us
  transfers between devices with their start and end apart: 6, of which 6 were waited for; matrix products, arithmetic and copies ran while one was open for 0% of the time, Pallas kernels for 5%

profile of v1, /device:TPU:4, one launch (start us, length us, event | category | flops | bytes accessed | tf_op | source)
XLA Modules:
  0.0 61.3 jit_solution(9018557171649066251)
XLA Ops:
  0.6 2.3 %send.1 = f32[128,8,128]{2,1,0:T(8,128)} custom-call(f32[512,128]{1,0:T(8,128)} %bitcast.21, f32[512,128]{1,0:T(8,128)} %bitcast.23, f32[512,128]{1,0:T(8,128)} %bitcast.25, f32[512,128]{1,0:T(8,128)} %bitcast.27), custom_call_target="tpu_custom_call" | custom-call | tf_op jit(solution)/shard_map/send/pallas_call | solution.py:274
  2.9 0.0 copy-start.11
  2.9 0.0 copy-start.4
  2.9 0.0 copy-start.6
  3.0 0.0 copy-start.9
  3.0 12.9 %all-to-all-start = ((f32[64,16,128]{2,1,0:T(8,128)}), f32[64,16,128]{2,1,0:T(8,128)S(1)}, u32[]{:S(2)}, u32[]{:S(2)}) async-start(f32[64,16,128]{2,1,0:T(8,128)} %bitcast.30), calls=%async_computation | async-start | bytes 1048576 | tf_op jit(solution)/shard_map/all_to_all | solution.py:284
  15.9 0.0 copy-start.7
  15.9 0.0 copy-done.11
  15.9 0.9 %collective-permute-start = (f32[128,128]{1,0:T(8,128)S(1)}, f32[128,128]{1,0:T(8,128)S(1)}, u32[]{:S(2)}, u32[]{:S(2)}) collective-permute-start(f32[128,128]{1,0:T(8,128)S(1)} %bitcast.31), channel_id=1, source_target_pairs={{0,128},{64,192},{128,0},{192,64},{1,129},{65,193},{129,1},{193,65... | collective-permute-start | bytes 196616 | tf_op jit(solution)/shard_map/ppermute | solution.py:268
  16.8 5.3 %collective-permute-done = f32[128,128]{1,0:T(8,128)S(1)} collective-permute-done((f32[128,128]{1,0:T(8,128)S(1)}, f32[128,128]{1,0:T(8,128)S(1)}, u32[]{:S(2)}, u32[]{:S(2)}) %collective-permute-start) | collective-permute-done | bytes 65568 | tf_op jit(solution)/shard_map/ppermute | solution.py:268
  22.1 0.1 collective-permute-start.1
  22.2 0.0 copy-start.5
  22.2 0.0 copy-start.8
  22.2 1.3 %collective-permute-done.1.far_ref = f32[256,128]{1,0:T(8,128)S(1)} collective-permute-done((f32[256,128]{1,0:T(8,128)S(1)}, f32[256,128]{1,0:T(8,128)S(1)}, u32[]{:S(2)}, u32[]{:S(2)}) %collective-permute-start.1) | collective-permute-done | bytes 131104 | tf_op jit(solution)/shard_map/ppermute | solution.py:268
  23.5 0.0 copy-done.4
  23.5 0.0 copy-done.6
  23.5 0.0 copy-done.9
  23.5 0.0 copy-done.7
  23.5 1.7 %taps.1.taps_ref = f32[2,256,256]{2,1,0:T(8,128)S(1)} custom-call(s32[4]{0:T(128)S(1)} %iota_xor_fusion.part_ref, f32[256,128]{1,0:T(8,128)S(1)} %pad_maximum_fusion.near_ref, f32[256,128]{1,0:T(8,128)S(1)} %collective-permute-done.1.far_ref, bf16[256,384]{1,0:T(8,128)(2,1)S(1)} %copy-done.9, f32[2,128,256]{2,1,0:T(8,128)S(1)} %copy-done.7, ...), custom_call_target="tpu_custom_call" | custom-call | flops 800000000 | bytes 1000000 | tf_op jit(solution)/shard_map/taps/pallas_call | solution.py:285
  25.3 8.2 %all-to-all-done = f32[64,16,128]{2,1,0:T(8,128)S(1)} async-done(((f32[64,16,128]{2,1,0:T(8,128)}), f32[64,16,128]{2,1,0:T(8,128)S(1)}, u32[]{:S(2)}, u32[]{:S(2)}) %all-to-all-start) | async-done | bytes 524320 | tf_op jit(solution)/shard_map/all_to_all | solution.py:284
  33.5 0.0 copy-done.5
  33.5 0.0 copy-done.8
  33.5 3.3 %spectral.1 = (f32[64,16,128]{2,1,0:T(8,128)}, f32[2,256,256]{2,1,0:T(8,128)}) custom-call(f32[1024,128]{1,0:T(8,128)S(1)} %bitcast.29, f32[2,256,256]{2,1,0:T(8,128)S(1)} %taps.1.taps_ref, bf16[256,384]{1,0:T(8,128)(2,1)S(1)} %copy-done.9, bf16[128,768]{1,0:T(8,128)(2,1)S(1)} %copy-done.8, f32[2,128,256]{2,1,0:T(8,128)S(1)} %copy-done.7, ...), custom_call_target="tpu_custom_call" | custom-call | flops 3200000000 | bytes 4000000 | tf_op jit(solution)/shard_map/spectral/pallas_call | solution.py:297
  36.8 0.0 copy-start.10
  36.8 6.2 %all-to-all-start.1 = ((f32[64,16,128]{2,1,0:T(8,128)}), f32[64,16,128]{2,1,0:T(8,128)S(1)}, u32[]{:S(2)}, u32[]{:S(2)}) async-start(f32[64,16,128]{2,1,0:T(8,128)} %get-tuple-element.12), calls=%async_computation.1 | async-start | bytes 1048576 | tf_op jit(solution)/shard_map/all_to_all | solution.py:310
  43.0 0.0 copy-done.10
  43.0 0.0 copy-start.2
  43.0 0.0 copy-start.3
  43.0 1.3 %terms.1 = (f32[256,128]{1,0:T(8,128)S(1)}, f32[256,128]{1,0:T(8,128)S(1)}) custom-call(s32[4]{0:T(128)S(1)} %iota_xor_fusion.part_ref, f32[2,256,256]{2,1,0:T(8,128)S(1)} %copy-done.10, bf16[128,768]{1,0:T(8,128)(2,1)S(1)} %copy-done.8, f32[2,128,256]{2,1,0:T(8,128)S(1)} %copy-done.7, bf16[768,256]{1,0:T(8,128)(2,1)S(1)} %copy-done.4, ...), custom_call_target="tpu_custom_call" | custom-call | flops 800000000 | bytes 1000000 | tf_op jit(solution)/shard_map/terms/pallas_call | solution.py:311
  44.2 0.1 collective-permute-start.2
  44.4 1.3 %collective-permute-done.2 = f32[256,128]{1,0:T(8,128)S(1)} collective-permute-done((f32[256,128]{1,0:T(8,128)S(1)}, f32[256,128]{1,0:T(8,128)S(1)}, u32[]{:S(2)}, u32[]{:S(2)}) %collective-permute-start.2) | collective-permute-done | bytes 131104 | tf_op jit(solution)/shard_map/ppermute | solution.py:268
  45.7 0.0 copy-start
  45.7 0.0 copy-start.1
  45.7 0.9 %collective-permute-start.3 = (f32[128,128]{1,0:T(8,128)S(1)}, f32[128,128]{1,0:T(8,128)S(1)}, u32[]{:S(2)}, u32[]{:S(2)}) collective-permute-start(f32[128,128]{1,0:T(8,128)S(1)} %get-tuple-element.20), channel_id=1, source_target_pairs={{0,128},{64,192},{128,0},{192,64},{1,129},{65,193},{129,1},{193,65... | collective-permute-start | bytes 196616 | tf_op jit(solution)/shard_map/ppermute | solution.py:268
  46.6 5.4 %collective-permute-done.3.far_ref = f32[128,128]{1,0:T(8,128)S(1)} collective-permute-done((f32[128,128]{1,0:T(8,128)S(1)}, f32[128,128]{1,0:T(8,128)S(1)}, u32[]{:S(2)}, u32[]{:S(2)}) %collective-permute-start.3) | collective-permute-done | bytes 65568 | tf_op jit(solution)/shard_map/ppermute | solution.py:268
  52.0 8.2 %all-to-all-done.1 = f32[64,16,128]{2,1,0:T(8,128)S(1)} async-done(((f32[64,16,128]{2,1,0:T(8,128)}), f32[64,16,128]{2,1,0:T(8,128)S(1)}, u32[]{:S(2)}, u32[]{:S(2)}) %all-to-all-start.1) | async-done | bytes 524320 | tf_op jit(solution)/shard_map/all_to_all | solution.py:310
  60.2 0.0 copy-done.2
  60.2 0.0 copy-done.3
  60.2 0.0 copy-done
  60.2 0.0 copy-done.1
  60.2 1.1 %finish.1 = (f32[512,128]{1,0:T(8,128)}, f32[512,128]{1,0:T(8,128)}, f32[512,128]{1,0:T(8,128)}, f32[128,128]{1,0:T(8,128)}) custom-call(f32[1024,128]{1,0:T(8,128)S(1)} %bitcast.20, f32[512,128]{1,0:T(8,128)S(1)} %bitcast.22, f32[512,128]{1,0:T(8,128)S(1)} %bitcast.24, f32[512,128]{1,0:T(8,128)S(1)} %bitcast.26, f32[512,128]{1,0:T(8,128)S(1)} %bitcast.28, ...), custom_call_target="tpu_custom_call" | custom-call | tf_op jit(solution)/shard_map/finish/pallas_call | solution.py:325
  (4 shorter events, 0.0 us)
Async XLA Ops:
  2.9 13.0 %copy-start.11 = (f32[2,8192]{1,0:T(2,128)S(1)}, f32[2,8192]{1,0:T(2,128)}, u32[]{:S(2)}) copy-start(f32[2,8192]{1,0:T(2,128)} %param.15) | copy-start | bytes 196612
  2.9 20.6 %copy-start.4 = (bf16[768,256]{1,0:T(8,128)(2,1)S(1)}, bf16[768,256]{1,0:T(8,128)(2,1)}, u32[]{:S(2)}) copy-start(bf16[768,256]{1,0:T(8,128)(2,1)} %constant.20.clone.te_ref) | copy-start | bytes 1179652
  2.9 20.6 %copy-start.6 = (bf16[768,256]{1,0:T(8,128)(2,1)S(1)}, bf16[768,256]{1,0:T(8,128)(2,1)}, u32[]{:S(2)}) copy-start(bf16[768,256]{1,0:T(8,128)(2,1)} %constant.21.clone.to_ref) | copy-start | bytes 1179652
  3.0 20.6 %copy-start.9 = (bf16[256,384]{1,0:T(8,128)(2,1)S(1)}, bf16[256,384]{1,0:T(8,128)(2,1)}, u32[]{:S(2)}) copy-start(bf16[256,384]{1,0:T(8,128)(2,1)} %constant.18.clone.wf_ref) | copy-start | bytes 589828
  3.0 30.5 %all-to-all-start = ((f32[64,16,128]{2,1,0:T(8,128)}), f32[64,16,128]{2,1,0:T(8,128)S(1)}, u32[]{:S(2)}, u32[]{:S(2)}) async-start(f32[64,16,128]{2,1,0:T(8,128)} %bitcast.30), calls=%async_computation | async-start | bytes 1048576 | tf_op jit(solution)/shard_map/all_to_all | solution.py:284
  15.9 7.7 %copy-start.7 = (f32[2,128,256]{2,1,0:T(8,128)S(1)}, f32[2,128,256]{2,1,0:T(8,128)}, u32[]{:S(2)}) copy-start(f32[2,128,256]{2,1,0:T(8,128)} %constant.19.clone.tw_ref) | copy-start | bytes 786436
  15.9 6.2 %collective-permute-start = (f32[128,128]{1,0:T(8,128)S(1)}, f32[128,128]{1,0:T(8,128)S(1)}, u32[]{:S(2)}, u32[]{:S(2)}) collective-permute-start(f32[128,128]{1,0:T(8,128)S(1)} %bitcast.31), channel_id=1, source_target_pairs={{0,128},{64,192},{128,0},{192,64},{1,129},{65,193},{129,1},{193,65... | collective-permute-start | bytes 196616 | tf_op jit(solution)/shard_map/ppermute | solution.py:268
  22.1 1.4 %collective-permute-start.1 = (f32[256,128]{1,0:T(8,128)S(1)}, f32[256,128]{1,0:T(8,128)S(1)}, u32[]{:S(2)}, u32[]{:S(2)}) collective-permute-start(f32[256,128]{1,0:T(8,128)S(1)} %pad_maximum_fusion.near_ref), channel_id=1, source_target_pairs={{0,64},{64,0},{128,192},{192,128},{1,65},{65,1},{129,193},{193,129... | collective-permute-start | bytes 393224 | tf_op jit(solution)/shard_map/ppermute | solution.py:268
  22.2 11.3 %copy-start.5 = (bf16[768,256]{1,0:T(8,128)(2,1)S(1)}, bf16[768,256]{1,0:T(8,128)(2,1)}, u32[]{:S(2)}) copy-start(bf16[768,256]{1,0:T(8,128)(2,1)} %constant.23.clone.tb_ref) | copy-start | bytes 1179652
  22.2 11.3 %copy-start.8 = (bf16[128,768]{1,0:T(8,128)(2,1)S(1)}, bf16[128,768]{1,0:T(8,128)(2,1)}, u32[]{:S(2)}) copy-start(bf16[128,768]{1,0:T(8,128)(2,1)} %constant.22.clone.wi_ref) | copy-start | bytes 589828
  36.8 6.2 %copy-start.10 = (f32[2,256,256]{2,1,0:T(8,128)S(1)}, f32[2,256,256]{2,1,0:T(8,128)}, u32[]{:S(2)}) copy-start(f32[2,256,256]{2,1,0:T(8,128)} %get-tuple-element.13.cross_ref) | copy-start | bytes 1572868
  36.8 23.4 %all-to-all-start.1 = ((f32[64,16,128]{2,1,0:T(8,128)}), f32[64,16,128]{2,1,0:T(8,128)S(1)}, u32[]{:S(2)}, u32[]{:S(2)}) async-start(f32[64,16,128]{2,1,0:T(8,128)} %get-tuple-element.12), calls=%async_computation.1 | async-start | bytes 1048576 | tf_op jit(solution)/shard_map/all_to_all | solution.py:310
  43.0 17.2 %copy-start.2 = (f32[1,512,128]{2,1,0:T(8,128)S(1)}, f32[1,512,128]{2,1,0:T(8,128)}, u32[]{:S(2)}) copy-start(f32[1,512,128]{2,1,0:T(8,128)} %param.13) | copy-start | bytes 786436
  43.0 17.2 %copy-start.3 = (f32[1,512,128]{2,1,0:T(8,128)S(1)}, f32[1,512,128]{2,1,0:T(8,128)}, u32[]{:S(2)}) copy-start(f32[1,512,128]{2,1,0:T(8,128)} %param.14) | copy-start | bytes 786436
  44.2 1.4 %collective-permute-start.2 = (f32[256,128]{1,0:T(8,128)S(1)}, f32[256,128]{1,0:T(8,128)S(1)}, u32[]{:S(2)}, u32[]{:S(2)}) collective-permute-start(f32[256,128]{1,0:T(8,128)S(1)} %get-tuple-element.15), channel_id=1, source_target_pairs={{0,64},{64,0},{128,192},{192,128},{1,65},{65,1},{129,193},{193,129... | collective-permute-start | bytes 393224 | tf_op jit(solution)/shard_map/ppermute | solution.py:268
  45.7 14.5 %copy-start = (f32[1,512,128]{2,1,0:T(8,128)S(1)}, f32[1,512,128]{2,1,0:T(8,128)}, u32[]{:S(2)}) copy-start(f32[1,512,128]{2,1,0:T(8,128)} %param.11) | copy-start | bytes 786436
  45.7 14.5 %copy-start.1 = (f32[1,512,128]{2,1,0:T(8,128)S(1)}, f32[1,512,128]{2,1,0:T(8,128)}, u32[]{:S(2)}) copy-start(f32[1,512,128]{2,1,0:T(8,128)} %param.12) | copy-start | bytes 786436
  45.7 6.3 %collective-permute-start.3 = (f32[128,128]{1,0:T(8,128)S(1)}, f32[128,128]{1,0:T(8,128)S(1)}, u32[]{:S(2)}, u32[]{:S(2)}) collective-permute-start(f32[128,128]{1,0:T(8,128)S(1)} %get-tuple-element.20), channel_id=1, source_target_pairs={{0,128},{64,192},{128,0},{192,64},{1,129},{65,193},{129,1},{193,65... | collective-permute-start | bytes 196616 | tf_op jit(solution)/shard_map/ppermute | solution.py:268

commit v2 on v1

--- a/solution.py
+++ b/solution.py
@@ -14,6 +14,7 @@
 OUTER = 128
 INNER = 256
 HALF = INNER // 2
+CHUNK = 16
 SCALE = LENGTH**-0.5 / LENGTH
 
 PIECE = (0, 2, 1, 3)
@@ -41,10 +42,11 @@
     k1 = np.arange(OUTER, dtype=np.float64)[:, None] + 0.25
     j = np.concatenate([np.arange(0, OUTER, 2), np.arange(1, OUTER, 2)]).astype(np.float64)[None, :]
     outer = 2.0 * np.pi * np.mod(k1 * j, OUTER) / OUTER
-    w = np.concatenate([np.cos(outer), -np.sin(outer)], axis=0)
+    w = np.stack([np.cos(outer), -np.sin(outer)]).reshape(2, OUTER // CHUNK, CHUNK, OUTER)
+    w = w.transpose(1, 0, 2, 3).reshape(2 * OUTER, OUTER)
     wh, wl = split_np(w)
     w_fwd = np.concatenate([wh, wh, wl], axis=1)
-    vh, vl = split_np(w.T)
+    vh, vl = split_np(w.T * SCALE)
     w_inv = np.concatenate([vh, vh, vl], axis=1)
     r = np.arange(INNER, dtype=np.float64)[None, :]
     twist = 2.0 * np.pi * k1 * r / LENGTH
@@ -86,10 +88,10 @@
         send.wait()
 
 
-def store_cat(cat, row, left, right):
+def store_cat(cat, first, left, right):
     lh, ll = split(left)
     rh, rl = split(right)
-    rows = pl.ds(row * OUTER, OUTER)
+    rows = pl.ds(first, left.shape[0])
     cat[rows, 0:128] = lh
     cat[rows, 128:256] = rh
     cat[rows, 256:384] = ll
@@ -101,24 +103,29 @@
 def forward_outer(x, row, wf_ref, tw_ref, cat_e, cat_o):
     xh, xl = split(x)
     a = jnp.dot(wf_ref[...], jnp.concatenate([xh, xl, xh], axis=0), preferred_element_type=f32)
-    ar, ai = a[:OUTER], a[OUTER:]
-    tr, ti = tw_ref[0], tw_ref[1]
-    br, bi = ar * tr - ai * ti, ar * ti + ai * tr
-    store_cat(cat_e, row, br[:, :HALF] + br[:, HALF:], bi[:, :HALF] + bi[:, HALF:])
-    store_cat(cat_o, row, br[:, :HALF] - br[:, HALF:], bi[:, :HALF] - bi[:, HALF:])
-
-
-def inverse_outer(spec_e, spec_o, row, wi_ref, tw_ref):
-    rows = pl.ds(row * OUTER, OUTER)
-    ei, er = spec_e[rows, 0:HALF], spec_e[rows, HALF : 2 * HALF]
-    oi, orr = spec_o[rows, 0:HALF], spec_o[rows, HALF : 2 * HALF]
-    dr = jnp.concatenate([er + orr, er - orr], axis=1)
-    di = jnp.concatenate([ei + oi, ei - oi], axis=1)
-    tr, ti = tw_ref[0], tw_ref[1]
-    e = jnp.concatenate([dr * tr + di * ti, di * tr - dr * ti], axis=0)
-    eh, el = split(e)
-    y = jnp.dot(wi_ref[...], jnp.concatenate([eh, el, eh], axis=0), preferred_element_type=f32)
-    return y * SCALE
+    for i in range(0, OUTER, CHUNK):
+        ar, ai = a[2 * i : 2 * i + CHUNK], a[2 * i + CHUNK : 2 * i + 2 * CHUNK]
+        tr, ti = tw_ref[0, i : i + CHUNK, :], tw_ref[1, i : i + CHUNK, :]
+        br, bi = ar * tr - ai * ti, ar * ti + ai * tr
+        first = row * OUTER + i
+        store_cat(cat_e, first, br[:, :HALF] + br[:, HALF:], bi[:, :HALF] + bi[:, HALF:])
+        store_cat(cat_o, first, br[:, :HALF] - br[:, HALF:], bi[:, :HALF] - bi[:, HALF:])
+
+
+def inverse_outer(spec_e, spec_o, row, wi_ref, tw_ref, cat):
+    for i in range(0, OUTER, CHUNK):
+        rows = pl.ds(row * OUTER + i, CHUNK)
+        ei, er = spec_e[rows, 0:HALF], spec_e[rows, HALF : 2 * HALF]
+        oi, orr = spec_o[rows, 0:HALF], spec_o[rows, HALF : 2 * HALF]
+        dr = jnp.concatenate([er + orr, er - orr], axis=1)
+        di = jnp.concatenate([ei + oi, ei - oi], axis=1)
+        tr, ti = tw_ref[0, i : i + CHUNK, :], tw_ref[1, i : i + CHUNK, :]
+        for first, e in ((2 * i, dr * tr + di * ti), (2 * i + CHUNK, di * tr - dr * ti)):
+            eh, el = split(e)
+            cat[pl.ds(first, CHUNK), :] = eh
+            cat[pl.ds(256 + first, CHUNK), :] = el
+            cat[pl.ds(512 + first, CHUNK), :] = eh
+    return matmul(wi_ref, cat)
 
 
 def matmul(cat, table):
@@ -151,10 +158,11 @@
 def spectral_kernel(
     recv_ref, taps_ref, wf_ref, wi_ref, tw_ref, te_ref, to_ref, tb_ref,
     out_hbm, cross_hbm,
-    cat_e, cat_o, spec_e, spec_o, cross, tiles, sem, out_sem,
+    cat_e, cat_o, spec_e, spec_o, back, cross, tiles, sem, out_sem,
 ):
-    for sig in range(2):
-        for c in range(2):
+    sends = []
+    for c in range(2):
+        for sig in range(2):
             x = jnp.concatenate(
                 [
                     jnp.concatenate(
@@ -165,32 +173,33 @@
                 ],
                 axis=0,
             )
-            forward_outer(x, 2 * sig + c, wf_ref, tw_ref, cat_e, cat_o)
+            forward_outer(x, 2 * c + sig, wf_ref, tw_ref, cat_e, cat_o)
+
+    def product(p, cat, spec):
+        for c in range(2):
+            for i in range(0, OUTER, CHUNK):
+                g, k = pl.ds(2 * c * OUTER + i, CHUNK), pl.ds((2 * c + 1) * OUTER + i, CHUNK)
+                h = pl.ds(c * OUTER + i, CHUNK)
+                gr, gi = spec[g, 0:HALF], spec[g, HALF : 2 * HALF]
+                cr, ci = spec[k, 0:HALF], spec[k, HALF : 2 * HALF]
+                hr, hi = taps_ref[p, h, 0:HALF], taps_ref[p, h, HALF : 2 * HALF]
+                store_cat(cat, 2 * c * OUTER + i, gr * hi + gi * hr, gr * hr - gi * hi)
+                store_cat(cat, (2 * c + 1) * OUTER + i, hr * ci - hi * cr, hr * cr + hi * ci)
+                cross[p, h, 0:HALF] = gr * ci - gi * cr
+                cross[p, h, HALF : 2 * HALF] = gr * cr + gi * ci
 
     spec_e[...] = matmul(cat_e, te_ref)
     spec_o[...] = matmul(cat_o, to_ref)
-
-    for p, (cat, spec) in enumerate(((cat_e, spec_e), (cat_o, spec_o))):
-        for c in range(2):
-            def part(ref, row, im):
-                return ref[pl.ds(row * OUTER, OUTER), pl.ds(im * HALF, HALF)]
-
-            gr, gi = part(spec, c, 0), part(spec, c, 1)
-            cr, ci = part(spec, 2 + c, 0), part(spec, 2 + c, 1)
-            hr, hi = part(taps_ref.at[p], c, 0), part(taps_ref.at[p], c, 1)
-            store_cat(cat, c, gr * hi + gi * hr, gr * hr - gi * hi)
-            store_cat(cat, 2 + c, hr * ci - hi * cr, hr * cr + hi * ci)
-            cross[p, pl.ds(c * OUTER, OUTER), 0:HALF] = gr * ci - gi * cr
-            cross[p, pl.ds(c * OUTER, OUTER), HALF : 2 * HALF] = gr * cr + gi * ci
-
-    sends = [pltpu.make_async_copy(cross, cross_hbm, sem)]
+    product(0, cat_e, spec_e)
+    spec_e[...] = matmul(cat_e, te_ref)
+    product(1, cat_o, spec_o)
+    sends.append(pltpu.make_async_copy(cross, cross_hbm, sem))
     sends[0].start()
-    spec_e[...] = matmul(cat_e, te_ref)
     spec_o[...] = matmul(cat_o, tb_ref)
 
-    for sig in range(2):
-        for c in range(2):
-            y = inverse_outer(spec_e, spec_o, 2 * sig + c, wi_ref, tw_ref)
+    for c in range(2):
+        for sig in range(2):
+            y = inverse_outer(spec_e, spec_o, 2 * c + sig, wi_ref, tw_ref, back.at[2 * c + sig])
             for q2 in range(2):
                 for h in range(2):
                     i = c * 8 + sig * 4 + 2 * q2 + h
@@ -202,16 +211,16 @@
 
 
 def terms_kernel(
-    part_ref, cross_ref, wi_ref, tw_ref, te_ref, tb_ref, own_ref, give_ref, cat_e, cat_o, spec_e, spec_o, terms
+    part_ref, cross_ref, wi_ref, tw_ref, te_ref, tb_ref, own_ref, give_ref, cat_e, cat_o, spec_e, spec_o, back, terms
 ):
     for p, cat in enumerate((cat_e, cat_o)):
         for c in range(2):
             rows = pl.ds(c * OUTER, OUTER)
-            store_cat(cat, c, cross_ref[p, rows, 0:HALF], cross_ref[p, rows, HALF : 2 * HALF])
+            store_cat(cat, c * OUTER, cross_ref[p, rows, 0:HALF], cross_ref[p, rows, HALF : 2 * HALF])
     spec_e[...] = matmul(cat_e, te_ref)
     spec_o[...] = matmul(cat_o, tb_ref)
     for c in range(2):
-        y = inverse_outer(spec_e, spec_o, c, wi_ref, tw_ref)
+        y = inverse_outer(spec_e, spec_o, c, wi_ref, tw_ref, back.at[c])
         for q2 in range(2):
             for h in range(2):
                 terms[pl.ds(4 * q2 + 2 * h + c, 64, stride=8), :] = y[
@@ -301,7 +310,7 @@
         out_specs=(HBM, HBM),
         scratch_shapes=[pltpu.VMEM((4 * OUTER, 3 * INNER), bf16)] * 2
         + [pltpu.VMEM((4 * OUTER, INNER), f32)] * 2
-        + [pltpu.VMEM((2, 2 * OUTER, INNER), f32)]
+        + [pltpu.VMEM((4, 6 * OUTER, INNER), bf16), pltpu.VMEM((2, 2 * OUTER, INNER), f32)]
         + [pltpu.VMEM((16, TOK, 128), f32), pltpu.SemaphoreType.DMA, pltpu.SemaphoreType.DMA((16,))],
         compiler_params=room(8),
         cost_estimate=cost(4),
@@ -315,7 +324,7 @@
         out_specs=(VMEM,) * 2,
         scratch_shapes=[pltpu.VMEM((2 * OUTER, 3 * INNER), bf16)] * 2
         + [pltpu.VMEM((2 * OUTER, INNER), f32)] * 2
-        + [pltpu.VMEM((SEQ * 128, 128), f32)],
+        + [pltpu.VMEM((2, 6 * OUTER, INNER), bf16), pltpu.VMEM((SEQ * 128, 128), f32)],
         compiler_params=room(8),
         cost_estimate=cost(1),
         name="terms",

time: 61.6 us -> 61.1 us (level)
  Pallas kernels: 9.6 us -> 8.98 us
where the time goes in v2:
time: 61.1 us; the launch traced here: 60.8 us
  waiting for transfers between devices  29.8 us (49%)
  starting transfers between devices  21 us (34%)
  Pallas kernels  8.98 us (15%)
  between operations  0.84 us (1%)
    ppermute x4, waiting for transfers between devices, swap(): return lax.ppermute(block, 'seq', [(s, s ^ k) for s in range(SEQ)])  13.3 us
    all_to_all x1, starting transfers between devices, body(): lax.all_to_all(sent.reshape(TOK, 16, 128), 'tok', split_axis=0, concat_ax...  12.9 us
    all_to_all x1, waiting for transfers between devices, body(): lax.all_to_all(sent.reshape(TOK, 16, 128), 'tok', split_axis=0, concat_ax...  8.3 us
    all_to_all x1, waiting for transfers between devices, body(): lax.all_to_all(back.reshape(TOK, 16, 128), 'tok', split_axis=0, concat_ax...  8.16 us
    all_to_all x1, starting transfers between devices, body(): lax.all_to_all(back.reshape(TOK, 16, 128), 'tok', split_axis=0, concat_ax...  6.19 us
    pallas_call x1, Pallas kernels, body(): pl.pallas_call(spectral_kernel, out_shape=(shape(TOK, 16, 128), pltpu.HBM...  2.74 us
    pallas_call x1, Pallas kernels, body(): pl.pallas_call(send_kernel, out_shape=shape(TOK * 2, 8, 128), in_specs=[H...  2.28 us
    ppermute x4, starting transfers between devices, swap(): return lax.ppermute(block, 'seq', [(s, s ^ k) for s in range(SEQ)])  1.95 us
  transfers between devices with their start and end apart: 6, of which 6 were waited for; matrix products, arithmetic and copies ran while one was open for 0% of the time, Pallas kernels for 5%

profile of v2, /device:TPU:4, one launch (start us, length us, event | category | flops | bytes accessed | tf_op | source)
XLA Modules:
  0.0 60.8 jit_solution(14882907308397747652)
XLA Ops:
  0.6 2.3 %send.1 = f32[128,8,128]{2,1,0:T(8,128)} custom-call(f32[512,128]{1,0:T(8,128)} %bitcast.21, f32[512,128]{1,0:T(8,128)} %bitcast.23, f32[512,128]{1,0:T(8,128)} %bitcast.25, f32[512,128]{1,0:T(8,128)} %bitcast.27), custom_call_target="tpu_custom_call" | custom-call | tf_op jit(solution)/shard_map/send/pallas_call | solution.py:283
  2.9 0.0 copy-start.11
  2.9 0.0 copy-start.4
  2.9 0.0 copy-start.6
  3.0 0.0 copy-start.9
  3.0 12.9 %all-to-all-start = ((f32[64,16,128]{2,1,0:T(8,128)}), f32[64,16,128]{2,1,0:T(8,128)S(1)}, u32[]{:S(2)}, u32[]{:S(2)}) async-start(f32[64,16,128]{2,1,0:T(8,128)} %bitcast.30), calls=%async_computation | async-start | bytes 1048576 | tf_op jit(solution)/shard_map/all_to_all | solution.py:293
  15.9 0.0 copy-start.7
  15.9 0.0 copy-done.11
  15.9 0.9 %collective-permute-start = (f32[128,128]{1,0:T(8,128)S(1)}, f32[128,128]{1,0:T(8,128)S(1)}, u32[]{:S(2)}, u32[]{:S(2)}) collective-permute-start(f32[128,128]{1,0:T(8,128)S(1)} %bitcast.31), channel_id=1, source_target_pairs={{0,128},{64,192},{128,0},{192,64},{1,129},{65,193},{129,1},{193,65... | collective-permute-start | bytes 196616 | tf_op jit(solution)/shard_map/ppermute | solution.py:277
  16.8 5.3 %collective-permute-done = f32[128,128]{1,0:T(8,128)S(1)} collective-permute-done((f32[128,128]{1,0:T(8,128)S(1)}, f32[128,128]{1,0:T(8,128)S(1)}, u32[]{:S(2)}, u32[]{:S(2)}) %collective-permute-start) | collective-permute-done | bytes 65568 | tf_op jit(solution)/shard_map/ppermute | solution.py:277
  22.1 0.1 collective-permute-start.1
  22.2 0.0 copy-start.5
  22.2 0.0 copy-start.8
  22.2 1.3 %collective-permute-done.1.far_ref = f32[256,128]{1,0:T(8,128)S(1)} collective-permute-done((f32[256,128]{1,0:T(8,128)S(1)}, f32[256,128]{1,0:T(8,128)S(1)}, u32[]{:S(2)}, u32[]{:S(2)}) %collective-permute-start.1) | collective-permute-done | bytes 131104 | tf_op jit(solution)/shard_map/ppermute | solution.py:277
  23.5 0.0 copy-done.4
  23.5 0.0 copy-done.6
  23.5 0.0 copy-done.9
  23.5 0.0 copy-done.7
  23.5 1.6 %taps.1.taps_ref = f32[2,256,256]{2,1,0:T(8,128)S(1)} custom-call(s32[4]{0:T(128)S(1)} %iota_xor_fusion.part_ref, f32[256,128]{1,0:T(8,128)S(1)} %pad_maximum_fusion.near_ref, f32[256,128]{1,0:T(8,128)S(1)} %collective-permute-done.1.far_ref, bf16[256,384]{1,0:T(8,128)(2,1)S(1)} %copy-done.9, f32[2,128,256]{2,1,0:T(8,128)S(1)} %copy-done.7, ...), custom_call_target="tpu_custom_call" | custom-call | flops 800000000 | bytes 1000000 | tf_op jit(solution)/shard_map/taps/pallas_call | solution.py:294
  25.2 8.3 %all-to-all-done = f32[64,16,128]{2,1,0:T(8,128)S(1)} async-done(((f32[64,16,128]{2,1,0:T(8,128)}), f32[64,16,128]{2,1,0:T(8,128)S(1)}, u32[]{:S(2)}, u32[]{:S(2)}) %all-to-all-start) | async-done | bytes 524320 | tf_op jit(solution)/shard_map/all_to_all | solution.py:293
  33.5 0.0 copy-done.5
  33.5 0.0 copy-done.8
  33.5 2.7 %spectral.1 = (f32[64,16,128]{2,1,0:T(8,128)}, f32[2,256,256]{2,1,0:T(8,128)}) custom-call(f32[1024,128]{1,0:T(8,128)S(1)} %bitcast.29, f32[2,256,256]{2,1,0:T(8,128)S(1)} %taps.1.taps_ref, bf16[256,384]{1,0:T(8,128)(2,1)S(1)} %copy-done.9, bf16[128,768]{1,0:T(8,128)(2,1)S(1)} %copy-done.8, f32[2,128,256]{2,1,0:T(8,128)S(1)} %copy-done.7, ...), custom_call_target="tpu_custom_call" | custom-call | flops 3200000000 | bytes 4000000 | tf_op jit(solution)/shard_map/spectral/pallas_call | solution.py:306
  36.2 0.0 copy-start.10
  36.2 6.2 %all-to-all-start.1 = ((f32[64,16,128]{2,1,0:T(8,128)}), f32[64,16,128]{2,1,0:T(8,128)S(1)}, u32[]{:S(2)}, u32[]{:S(2)}) async-start(f32[64,16,128]{2,1,0:T(8,128)} %get-tuple-element.12), calls=%async_computation.1 | async-start | bytes 1048576 | tf_op jit(solution)/shard_map/all_to_all | solution.py:319
  42.4 0.0 copy-done.10
  42.4 0.0 copy-start.2
  42.5 0.0 copy-start.3
  42.5 1.3 %terms.1 = (f32[256,128]{1,0:T(8,128)S(1)}, f32[256,128]{1,0:T(8,128)S(1)}) custom-call(s32[4]{0:T(128)S(1)} %iota_xor_fusion.part_ref, f32[2,256,256]{2,1,0:T(8,128)S(1)} %copy-done.10, bf16[128,768]{1,0:T(8,128)(2,1)S(1)} %copy-done.8, f32[2,128,256]{2,1,0:T(8,128)S(1)} %copy-done.7, bf16[768,256]{1,0:T(8,128)(2,1)S(1)} %copy-done.4, ...), custom_call_target="tpu_custom_call" | custom-call | flops 800000000 | bytes 1000000 | tf_op jit(solution)/shard_map/terms/pallas_call | solution.py:320
  43.7 0.1 collective-permute-start.2
  43.8 1.3 %collective-permute-done.2 = f32[256,128]{1,0:T(8,128)S(1)} collective-permute-done((f32[256,128]{1,0:T(8,128)S(1)}, f32[256,128]{1,0:T(8,128)S(1)}, u32[]{:S(2)}, u32[]{:S(2)}) %collective-permute-start.2) | collective-permute-done | bytes 131104 | tf_op jit(solution)/shard_map/ppermute | solution.py:277
  45.2 0.0 copy-start
  45.2 0.0 copy-start.1
  45.2 0.9 %collective-permute-start.3 = (f32[128,128]{1,0:T(8,128)S(1)}, f32[128,128]{1,0:T(8,128)S(1)}, u32[]{:S(2)}, u32[]{:S(2)}) collective-permute-start(f32[128,128]{1,0:T(8,128)S(1)} %get-tuple-element.20), channel_id=1, source_target_pairs={{0,128},{64,192},{128,0},{192,64},{1,129},{65,193},{129,1},{193,65... | collective-permute-start | bytes 196616 | tf_op jit(solution)/shard_map/ppermute | solution.py:277
  46.1 5.4 %collective-permute-done.3.far_ref = f32[128,128]{1,0:T(8,128)S(1)} collective-permute-done((f32[128,128]{1,0:T(8,128)S(1)}, f32[128,128]{1,0:T(8,128)S(1)}, u32[]{:S(2)}, u32[]{:S(2)}) %collective-permute-start.3) | collective-permute-done | bytes 65568 | tf_op jit(solution)/shard_map/ppermute | solution.py:277
  51.5 8.2 %all-to-all-done.1 = f32[64,16,128]{2,1,0:T(8,128)S(1)} async-done(((f32[64,16,128]{2,1,0:T(8,128)}), f32[64,16,128]{2,1,0:T(8,128)S(1)}, u32[]{:S(2)}, u32[]{:S(2)}) %all-to-all-start.1) | async-done | bytes 524320 | tf_op jit(solution)/shard_map/all_to_all | solution.py:319
  59.7 0.0 copy-done.2
  59.7 0.0 copy-done.3
  59.7 0.0 copy-done
  59.7 0.0 copy-done.1
  59.7 1.1 %finish.1 = (f32[512,128]{1,0:T(8,128)}, f32[512,128]{1,0:T(8,128)}, f32[512,128]{1,0:T(8,128)}, f32[128,128]{1,0:T(8,128)}) custom-call(f32[1024,128]{1,0:T(8,128)S(1)} %bitcast.20, f32[512,128]{1,0:T(8,128)S(1)} %bitcast.22, f32[512,128]{1,0:T(8,128)S(1)} %bitcast.24, f32[512,128]{1,0:T(8,128)S(1)} %bitcast.26, f32[512,128]{1,0:T(8,128)S(1)} %bitcast.28, ...), custom_call_target="tpu_custom_call" | custom-call | tf_op jit(solution)/shard_map/finish/pallas_call | solution.py:334
  (4 shorter events, 0.0 us)
Async XLA Ops:
  2.9 13.0 %copy-start.11 = (f32[2,8192]{1,0:T(2,128)S(1)}, f32[2,8192]{1,0:T(2,128)}, u32[]{:S(2)}) copy-start(f32[2,8192]{1,0:T(2,128)} %param.15) | copy-start | bytes 196612
  2.9 20.6 %copy-start.4 = (bf16[768,256]{1,0:T(8,128)(2,1)S(1)}, bf16[768,256]{1,0:T(8,128)(2,1)}, u32[]{:S(2)}) copy-start(bf16[768,256]{1,0:T(8,128)(2,1)} %constant.20.clone.te_ref) | copy-start | bytes 1179652
  2.9 20.6 %copy-start.6 = (bf16[768,256]{1,0:T(8,128)(2,1)S(1)}, bf16[768,256]{1,0:T(8,128)(2,1)}, u32[]{:S(2)}) copy-start(bf16[768,256]{1,0:T(8,128)(2,1)} %constant.21.clone.to_ref) | copy-start | bytes 1179652
  3.0 20.6 %copy-start.9 = (bf16[256,384]{1,0:T(8,128)(2,1)S(1)}, bf16[256,384]{1,0:T(8,128)(2,1)}, u32[]{:S(2)}) copy-start(bf16[256,384]{1,0:T(8,128)(2,1)} %constant.18.clone.wf_ref) | copy-start | bytes 589828
  3.0 30.5 %all-to-all-start = ((f32[64,16,128]{2,1,0:T(8,128)}), f32[64,16,128]{2,1,0:T(8,128)S(1)}, u32[]{:S(2)}, u32[]{:S(2)}) async-start(f32[64,16,128]{2,1,0:T(8,128)} %bitcast.30), calls=%async_computation | async-start | bytes 1048576 | tf_op jit(solution)/shard_map/all_to_all | solution.py:293
  15.9 7.7 %copy-start.7 = (f32[2,128,256]{2,1,0:T(8,128)S(1)}, f32[2,128,256]{2,1,0:T(8,128)}, u32[]{:S(2)}) copy-start(f32[2,128,256]{2,1,0:T(8,128)} %constant.19.clone.tw_ref) | copy-start | bytes 786436
  15.9 6.2 %collective-permute-start = (f32[128,128]{1,0:T(8,128)S(1)}, f32[128,128]{1,0:T(8,128)S(1)}, u32[]{:S(2)}, u32[]{:S(2)}) collective-permute-start(f32[128,128]{1,0:T(8,128)S(1)} %bitcast.31), channel_id=1, source_target_pairs={{0,128},{64,192},{128,0},{192,64},{1,129},{65,193},{129,1},{193,65... | collective-permute-start | bytes 196616 | tf_op jit(solution)/shard_map/ppermute | solution.py:277
  22.1 1.4 %collective-permute-start.1 = (f32[256,128]{1,0:T(8,128)S(1)}, f32[256,128]{1,0:T(8,128)S(1)}, u32[]{:S(2)}, u32[]{:S(2)}) collective-permute-start(f32[256,128]{1,0:T(8,128)S(1)} %pad_maximum_fusion.near_ref), channel_id=1, source_target_pairs={{0,64},{64,0},{128,192},{192,128},{1,65},{65,1},{129,193},{193,129... | collective-permute-start | bytes 393224 | tf_op jit(solution)/shard_map/ppermute | solution.py:277
  22.2 11.3 %copy-start.5 = (bf16[768,256]{1,0:T(8,128)(2,1)S(1)}, bf16[768,256]{1,0:T(8,128)(2,1)}, u32[]{:S(2)}) copy-start(bf16[768,256]{1,0:T(8,128)(2,1)} %constant.23.clone.tb_ref) | copy-start | bytes 1179652
  22.2 11.3 %copy-start.8 = (bf16[128,768]{1,0:T(8,128)(2,1)S(1)}, bf16[128,768]{1,0:T(8,128)(2,1)}, u32[]{:S(2)}) copy-start(bf16[128,768]{1,0:T(8,128)(2,1)} %constant.22.clone.wi_ref) | copy-start | bytes 589828
  36.2 6.2 %copy-start.10 = (f32[2,256,256]{2,1,0:T(8,128)S(1)}, f32[2,256,256]{2,1,0:T(8,128)}, u32[]{:S(2)}) copy-start(f32[2,256,256]{2,1,0:T(8,128)} %get-tuple-element.13.cross_ref) | copy-start | bytes 1572868
  36.2 23.4 %all-to-all-start.1 = ((f32[64,16,128]{2,1,0:T(8,128)}), f32[64,16,128]{2,1,0:T(8,128)S(1)}, u32[]{:S(2)}, u32[]{:S(2)}) async-start(f32[64,16,128]{2,1,0:T(8,128)} %get-tuple-element.12), calls=%async_computation.1 | async-start | bytes 1048576 | tf_op jit(solution)/shard_map/all_to_all | solution.py:319
  42.4 17.2 %copy-start.2 = (f32[1,512,128]{2,1,0:T(8,128)S(1)}, f32[1,512,128]{2,1,0:T(8,128)}, u32[]{:S(2)}) copy-start(f32[1,512,128]{2,1,0:T(8,128)} %param.13) | copy-start | bytes 786436
  42.5 17.2 %copy-start.3 = (f32[1,512,128]{2,1,0:T(8,128)S(1)}, f32[1,512,128]{2,1,0:T(8,128)}, u32[]{:S(2)}) copy-start(f32[1,512,128]{2,1,0:T(8,128)} %param.14) | copy-start | bytes 786436
  43.7 1.4 %collective-permute-start.2 = (f32[256,128]{1,0:T(8,128)S(1)}, f32[256,128]{1,0:T(8,128)S(1)}, u32[]{:S(2)}, u32[]{:S(2)}) collective-permute-start(f32[256,128]{1,0:T(8,128)S(1)} %get-tuple-element.15), channel_id=1, source_target_pairs={{0,64},{64,0},{128,192},{192,128},{1,65},{65,1},{129,193},{193,129... | collective-permute-start | bytes 393224 | tf_op jit(solution)/shard_map/ppermute | solution.py:277
  45.2 14.5 %copy-start = (f32[1,512,128]{2,1,0:T(8,128)S(1)}, f32[1,512,128]{2,1,0:T(8,128)}, u32[]{:S(2)}) copy-start(f32[1,512,128]{2,1,0:T(8,128)} %param.11) | copy-start | bytes 786436
  45.2 14.5 %copy-start.1 = (f32[1,512,128]{2,1,0:T(8,128)S(1)}, f32[1,512,128]{2,1,0:T(8,128)}, u32[]{:S(2)}) copy-start(f32[1,512,128]{2,1,0:T(8,128)} %param.12) | copy-start | bytes 786436
  45.2 6.3 %collective-permute-start.3 = (f32[128,128]{1,0:T(8,128)S(1)}, f32[128,128]{1,0:T(8,128)S(1)}, u32[]{:S(2)}, u32[]{:S(2)}) collective-permute-start(f32[128,128]{1,0:T(8,128)S(1)} %get-tuple-element.20), channel_id=1, source_target_pairs={{0,128},{64,192},{128,0},{192,64},{1,129},{65,193},{129,1},{193,65... | collective-permute-start | bytes 196616 | tf_op jit(solution)/shard_map/ppermute | solution.py:277

commit v3 on v2

--- a/solution.py
+++ b/solution.py
@@ -8,6 +8,8 @@
 
 TOK = 64
 SEQ = 4
+FIRST_OUT = 42
+FIRST_HOME = 42
 ROWS = 512
 WIDTH = 128
 LENGTH = TOK * ROWS
@@ -33,6 +35,20 @@
     return high, low
 
 
+def order(first):
+    devices = list(range(TOK))
+    devices[0], devices[first] = first, 0
+    return devices
+
+
+def swap_rows(ref, first, second, size):
+    if first == second:
+        return
+    a, b = ref[pl.ds(first, size), :], ref[pl.ds(second, size), :]
+    ref[pl.ds(first, size), :] = b
+    ref[pl.ds(second, size), :] = a
+
+
 def stack_np(real, imag, left):
     high, low = split_np(np.block([[real, imag], [-imag, real]]))
     return np.concatenate([high, high, low], axis=1 if left else 0)
@@ -40,13 +56,17 @@
 
 def tables():
     k1 = np.arange(OUTER, dtype=np.float64)[:, None] + 0.25
-    j = np.concatenate([np.arange(0, OUTER, 2), np.arange(1, OUTER, 2)]).astype(np.float64)[None, :]
-    outer = 2.0 * np.pi * np.mod(k1 * j, OUTER) / OUTER
-    w = np.stack([np.cos(outer), -np.sin(outer)]).reshape(2, OUTER // CHUNK, CHUNK, OUTER)
-    w = w.transpose(1, 0, 2, 3).reshape(2 * OUTER, OUTER)
-    wh, wl = split_np(w)
+
+    def outer_table(first):
+        block = np.array(order(first))
+        j = np.concatenate([2 * block, 2 * block + 1]).astype(np.float64)[None, :]
+        outer = 2.0 * np.pi * np.mod(k1 * j, OUTER) / OUTER
+        w = np.stack([np.cos(outer), -np.sin(outer)]).reshape(2, OUTER // CHUNK, CHUNK, OUTER)
+        return w.transpose(1, 0, 2, 3).reshape(2 * OUTER, OUTER)
+
+    wh, wl = split_np(outer_table(FIRST_OUT))
     w_fwd = np.concatenate([wh, wh, wl], axis=1)
-    vh, vl = split_np(w.T * SCALE)
+    vh, vl = split_np(outer_table(FIRST_HOME).T * SCALE)
     w_inv = np.concatenate([vh, vh, vl], axis=1)
     r = np.arange(INNER, dtype=np.float64)[None, :]
     twist = 2.0 * np.pi * k1 * r / LENGTH
@@ -82,6 +102,7 @@
         tiles[q] = (key[rows, :] * value[rows, :]).T
         tiles[4 + q] = (grad[rows, :] * query[rows, :]).T
         for i in (q, 4 + q):
+            swap_rows(tiles.at[i], 0, 2 * FIRST_OUT, 2)
             sends.append(pltpu.make_async_copy(tiles.at[i], out_hbm.at[:, i, :], out_sem.at[i]))
             sends[-1].start()
     for send in sends:
@@ -145,6 +166,8 @@
                         pl.ds(first + 4 * q2 + 2 * h + c, 16, stride=8), :
                     ]
     for c in range(2):
+        for q2 in range(2):
+            swap_rows(taps.at[c], 64 * q2, 64 * q2 + FIRST_OUT, 1)
         forward_outer(taps[c], c, wf_ref, tw_ref, cat_e, cat_o)
     copies = []
     for p, (cat, t_ref) in enumerate(((cat_e, te_ref), (cat_o, to_ref))):
@@ -226,6 +249,7 @@
                 terms[pl.ds(4 * q2 + 2 * h + c, 64, stride=8), :] = y[
                     q2 * 64 : q2 * 64 + 64, h * 128 : h * 128 + 128
                 ]
+    swap_rows(terms, 0, 8 * FIRST_HOME, 8)
     for k in range(SEQ):
         ref, first = (own_ref if k < 2 else give_ref), (k % 2) * 128
         ref[first : first + 128, :] = terms[
@@ -236,15 +260,17 @@
 def finish_kernel(
     recv_ref, query_ref, key_ref, value_ref, grad_ref, own_ref, far_ref,
     qg_hbm, kg_hbm, vg_hbm, fg_hbm,
-    qg, kg, vg, fg, sem,
+    qg, kg, vg, fg, tiles, sem,
 ):
     fg[...] = own_ref[...] + far_ref[...]
     copies = [pltpu.make_async_copy(fg, fg_hbm, sem.at[12])]
     copies[0].start()
     for q in range(4):
         rows = pl.ds(q * 128, 128)
-        conv = recv_ref[pl.ds(q, 128, stride=8), :].T
-        ggrad = recv_ref[pl.ds(4 + q, 128, stride=8), :].T
+        for i in (q, 4 + q):
+            tiles[i] = recv_ref[pl.ds(i, 128, stride=8), :]
+            swap_rows(tiles.at[i], 0, 2 * FIRST_HOME, 2)
+        conv, ggrad = tiles[q].T, tiles[4 + q].T
         qg[rows, :] = grad_ref[rows, :] * conv
         kg[rows, :] = ggrad * value_ref[rows, :]
         vg[rows, :] = ggrad * key_ref[rows, :]
@@ -275,6 +301,16 @@
 
     def swap(block, k):
         return lax.ppermute(block, "seq", [(s, s ^ k) for s in range(SEQ)])
+
+    def exchange(block, first):
+        return lax.all_to_all(
+            block.reshape(TOK, 16, 128),
+            "tok",
+            split_axis=0,
+            concat_axis=0,
+            tiled=True,
+            axis_index_groups=[order(first)],
+        )
 
     own = filter_param.reshape(2, 64, 128).transpose(1, 0, 2).reshape(128, 128)
     near = jnp.concatenate([own, swap(own, 2)], axis=0)
@@ -290,7 +326,7 @@
         compiler_params=room(60),
         name="send",
     )(query, key, value, grad)
-    recv = lax.all_to_all(sent.reshape(TOK, 16, 128), "tok", split_axis=0, concat_axis=0, tiled=True)
+    recv = exchange(sent, FIRST_OUT)
     taps = pl.pallas_call(
         taps_kernel,
         out_shape=shape(2, 2 * OUTER, INNER),
@@ -316,7 +352,7 @@
         cost_estimate=cost(4),
         name="spectral",
     )(recv.reshape(TOK * 16, 128), taps, w_fwd, w_inv, tw, t_even, t_odd, t_back)
-    home = lax.all_to_all(back.reshape(TOK, 16, 128), "tok", split_axis=0, concat_axis=0, tiled=True)
+    home = exchange(back, FIRST_HOME)
     kept, given = pl.pallas_call(
         terms_kernel,
         out_shape=(shape(256, 128),) * 2,
@@ -337,7 +373,7 @@
         in_specs=[VMEM] * 7,
         out_specs=(HBM,) * 4,
         scratch_shapes=[pltpu.VMEM((ROWS, WIDTH), f32)] * 3
-        + [pltpu.VMEM((128, 128), f32), pltpu.SemaphoreType.DMA((13,))],
+        + [pltpu.VMEM((128, 128), f32), pltpu.VMEM((8, 128, 128), f32), pltpu.SemaphoreType.DMA((13,))],
         compiler_params=room(8),
         name="finish",
     )(home.reshape(TOK * 16, 128), query, key, value, grad, *terms)

time: 61.1 us -> 57.2 us (0.936)
  waiting for transfers between devices: 29.8 us -> 19.6 us
  starting transfers between devices: 21 us -> 27.2 us
    all_to_all x2, waiting for transfers between devices: 16.5 us -> 5.33 us  [exchange(): lax.all_to_all(block.reshape(TOK, 16, 128), 'tok', split_axis=0, concat_a...]
    all_to_all x2, starting transfers between devices: 19.1 us -> 25.3 us  [exchange(): lax.all_to_all(block.reshape(TOK, 16, 128), 'tok', split_axis=0, concat_a...]
    ppermute x4, waiting for transfers between devices: 13.3 us -> 14.2 us  [swap(): return lax.ppermute(block, 'seq', [(s, s ^ k) for s in range(SEQ)])]
where the time goes in v3:
time: 57.2 us; the launch traced here: 56.8 us
  starting transfers between devices  27.2 us (48%)
  waiting for transfers between devices  19.6 us (34%)
  Pallas kernels  9.04 us (16%)
  between operations  0.84 us (1%)
    all_to_all x2, starting transfers between devices, exchange(): lax.all_to_all(block.reshape(TOK, 16, 128), 'tok', split_axis=0, concat_a...  25.3 us
    ppermute x4, waiting for transfers between devices, swap(): return lax.ppermute(block, 'seq', [(s, s ^ k) for s in range(SEQ)])  14.2 us
    all_to_all x2, waiting for transfers between devices, exchange(): lax.all_to_all(block.reshape(TOK, 16, 128), 'tok', split_axis=0, concat_a...  5.33 us
    pallas_call x1, Pallas kernels, body(): pl.pallas_call(spectral_kernel, out_shape=(shape(TOK, 16, 128), pltpu.HBM...  2.74 us
    pallas_call x1, Pallas kernels, body(): pl.pallas_call(send_kernel, out_shape=shape(TOK * 2, 8, 128), in_specs=[H...  2.29 us
    ppermute x4, starting transfers between devices, swap(): return lax.ppermute(block, 'seq', [(s, s ^ k) for s in range(SEQ)])  1.96 us
    pallas_call x1, Pallas kernels, body(): pl.pallas_call(taps_kernel, out_shape=shape(2, 2 * OUTER, INNER), in_spec...  1.64 us
    pallas_call x1, Pallas kernels, body(): pl.pallas_call(terms_kernel, out_shape=(shape(256, 128),) * 2, in_specs=[...  1.26 us
  transfers between devices with their start and end apart: 6, of which 6 were waited for; matrix products, arithmetic and copies ran while one was open for 0% of the time, Pallas kernels for 5%

profile of v3, /device:TPU:4, one launch (start us, length us, event | category | flops | bytes accessed | tf_op | source)
XLA Modules:
  0.0 56.8 jit_solution(17955835570889052435)
XLA Ops:
  0.6 2.3 %send.1 = f32[128,8,128]{2,1,0:T(8,128)} custom-call(f32[512,128]{1,0:T(8,128)} %bitcast.21, f32[512,128]{1,0:T(8,128)} %bitcast.23, f32[512,128]{1,0:T(8,128)} %bitcast.25, f32[512,128]{1,0:T(8,128)} %bitcast.27), custom_call_target="tpu_custom_call" | custom-call | tf_op jit(solution)/shard_map/send/pallas_call | solution.py:319
  2.9 0.0 copy-start.11
  2.9 0.0 copy-start.4
  3.0 0.0 copy-start.6
  3.0 0.0 copy-start.9
  3.0 14.3 %all-to-all-start = ((f32[64,16,128]{2,1,0:T(8,128)}), f32[64,16,128]{2,1,0:T(8,128)S(1)}, u32[]{:S(2)}, u32[]{:S(2)}) async-start(f32[64,16,128]{2,1,0:T(8,128)} %bitcast.30), calls=%async_computation | async-start | bytes 1048576 | tf_op jit(solution)/shard_map/all_to_all | solution.py:306
  17.3 0.0 copy-start.7
  17.3 0.0 copy-done.11
  17.3 0.9 %collective-permute-start = (f32[128,128]{1,0:T(8,128)S(1)}, f32[128,128]{1,0:T(8,128)S(1)}, u32[]{:S(2)}, u32[]{:S(2)}) collective-permute-start(f32[128,128]{1,0:T(8,128)S(1)} %bitcast.31), channel_id=1, source_target_pairs={{0,128},{64,192},{128,0},{192,64},{1,129},{65,193},{129,1},{193,65... | collective-permute-start | bytes 196616 | tf_op jit(solution)/shard_map/ppermute | solution.py:303
  18.2 5.5 %collective-permute-done = f32[128,128]{1,0:T(8,128)S(1)} collective-permute-done((f32[128,128]{1,0:T(8,128)S(1)}, f32[128,128]{1,0:T(8,128)S(1)}, u32[]{:S(2)}, u32[]{:S(2)}) %collective-permute-start) | collective-permute-done | bytes 65568 | tf_op jit(solution)/shard_map/ppermute | solution.py:303
  23.8 0.1 collective-permute-start.1
  23.9 0.0 copy-start.5
  23.9 0.0 copy-start.8
  23.9 1.3 %collective-permute-done.1.far_ref = f32[256,128]{1,0:T(8,128)S(1)} collective-permute-done((f32[256,128]{1,0:T(8,128)S(1)}, f32[256,128]{1,0:T(8,128)S(1)}, u32[]{:S(2)}, u32[]{:S(2)}) %collective-permute-start.1) | collective-permute-done | bytes 131104 | tf_op jit(solution)/shard_map/ppermute | solution.py:303
  25.2 0.0 copy-done.4
  25.2 0.0 copy-done.6
  25.2 0.0 copy-done.9
  25.2 0.0 copy-done.7
  25.2 1.6 %taps.1.taps_ref = f32[2,256,256]{2,1,0:T(8,128)S(1)} custom-call(s32[4]{0:T(128)S(1)} %iota_xor_fusion.part_ref, f32[256,128]{1,0:T(8,128)S(1)} %pad_maximum_fusion.near_ref, f32[256,128]{1,0:T(8,128)S(1)} %collective-permute-done.1.far_ref, bf16[256,384]{1,0:T(8,128)(2,1)S(1)} %copy-done.9, f32[2,128,256]{2,1,0:T(8,128)S(1)} %copy-done.7, ...), custom_call_target="tpu_custom_call" | custom-call | flops 800000000 | bytes 1000000 | tf_op jit(solution)/shard_map/taps/pallas_call | solution.py:330
  26.9 3.1 %all-to-all-done = f32[64,16,128]{2,1,0:T(8,128)S(1)} async-done(((f32[64,16,128]{2,1,0:T(8,128)}), f32[64,16,128]{2,1,0:T(8,128)S(1)}, u32[]{:S(2)}, u32[]{:S(2)}) %all-to-all-start) | async-done | bytes 524320 | tf_op jit(solution)/shard_map/all_to_all | solution.py:306
  30.0 0.0 copy-done.5
  30.0 0.0 copy-done.8
  30.0 2.7 %spectral.1 = (f32[64,16,128]{2,1,0:T(8,128)}, f32[2,256,256]{2,1,0:T(8,128)}) custom-call(f32[1024,128]{1,0:T(8,128)S(1)} %bitcast.29, f32[2,256,256]{2,1,0:T(8,128)S(1)} %taps.1.taps_ref, bf16[256,384]{1,0:T(8,128)(2,1)S(1)} %copy-done.9, bf16[128,768]{1,0:T(8,128)(2,1)S(1)} %copy-done.8, f32[2,128,256]{2,1,0:T(8,128)S(1)} %copy-done.7, ...), custom_call_target="tpu_custom_call" | custom-call | flops 3200000000 | bytes 4000000 | tf_op jit(solution)/shard_map/spectral/pallas_call | solution.py:342
  32.7 0.0 copy-start.10
  32.8 10.9 %all-to-all-start.1 = ((f32[64,16,128]{2,1,0:T(8,128)}), f32[64,16,128]{2,1,0:T(8,128)S(1)}, u32[]{:S(2)}, u32[]{:S(2)}) async-start(f32[64,16,128]{2,1,0:T(8,128)} %get-tuple-element.12), calls=%async_computation.1 | async-start | bytes 1048576 | tf_op jit(solution)/shard_map/all_to_all | solution.py:306
  43.7 0.0 copy-done.10
  43.7 0.0 copy-start.2
  43.7 0.0 copy-start.3
  43.7 1.3 %terms.1 = (f32[256,128]{1,0:T(8,128)S(1)}, f32[256,128]{1,0:T(8,128)S(1)}) custom-call(s32[4]{0:T(128)S(1)} %iota_xor_fusion.part_ref, f32[2,256,256]{2,1,0:T(8,128)S(1)} %copy-done.10, bf16[128,768]{1,0:T(8,128)(2,1)S(1)} %copy-done.8, f32[2,128,256]{2,1,0:T(8,128)S(1)} %copy-done.7, bf16[768,256]{1,0:T(8,128)(2,1)S(1)} %copy-done.4, ...), custom_call_target="tpu_custom_call" | custom-call | flops 800000000 | bytes 1000000 | tf_op jit(solution)/shard_map/terms/pallas_call | solution.py:356
  45.0 0.1 collective-permute-start.2
  45.1 1.3 %collective-permute-done.2 = f32[256,128]{1,0:T(8,128)S(1)} collective-permute-done((f32[256,128]{1,0:T(8,128)S(1)}, f32[256,128]{1,0:T(8,128)S(1)}, u32[]{:S(2)}, u32[]{:S(2)}) %collective-permute-start.2) | collective-permute-done | bytes 131104 | tf_op jit(solution)/shard_map/ppermute | solution.py:303
  46.4 0.0 copy-start
  46.4 0.0 copy-start.1
  46.5 0.9 %collective-permute-start.3 = (f32[128,128]{1,0:T(8,128)S(1)}, f32[128,128]{1,0:T(8,128)S(1)}, u32[]{:S(2)}, u32[]{:S(2)}) collective-permute-start(f32[128,128]{1,0:T(8,128)S(1)} %get-tuple-element.20), channel_id=1, source_target_pairs={{0,128},{64,192},{128,0},{192,64},{1,129},{65,193},{129,1},{193,65... | collective-permute-start | bytes 196616 | tf_op jit(solution)/shard_map/ppermute | solution.py:303
  47.3 6.1 %collective-permute-done.3.far_ref = f32[128,128]{1,0:T(8,128)S(1)} collective-permute-done((f32[128,128]{1,0:T(8,128)S(1)}, f32[128,128]{1,0:T(8,128)S(1)}, u32[]{:S(2)}, u32[]{:S(2)}) %collective-permute-start.3) | collective-permute-done | bytes 65568 | tf_op jit(solution)/shard_map/ppermute | solution.py:303
  53.4 2.2 %all-to-all-done.1 = f32[64,16,128]{2,1,0:T(8,128)S(1)} async-done(((f32[64,16,128]{2,1,0:T(8,128)}), f32[64,16,128]{2,1,0:T(8,128)S(1)}, u32[]{:S(2)}, u32[]{:S(2)}) %all-to-all-start.1) | async-done | bytes 524320 | tf_op jit(solution)/shard_map/all_to_all | solution.py:306
  55.6 0.0 copy-done.2
  55.6 0.0 copy-done.3
  55.7 0.0 copy-done
  55.7 0.0 copy-done.1
  55.7 1.1 %finish.1 = (f32[512,128]{1,0:T(8,128)}, f32[512,128]{1,0:T(8,128)}, f32[512,128]{1,0:T(8,128)}, f32[128,128]{1,0:T(8,128)}) custom-call(f32[1024,128]{1,0:T(8,128)S(1)} %bitcast.20, f32[512,128]{1,0:T(8,128)S(1)} %bitcast.22, f32[512,128]{1,0:T(8,128)S(1)} %bitcast.24, f32[512,128]{1,0:T(8,128)S(1)} %bitcast.26, f32[512,128]{1,0:T(8,128)S(1)} %bitcast.28, ...), custom_call_target="tpu_custom_call" | custom-call | tf_op jit(solution)/shard_map/finish/pallas_call | solution.py:370
  (4 shorter events, 0.0 us)
Async XLA Ops:
  2.9 14.4 %copy-start.11 = (f32[2,8192]{1,0:T(2,128)S(1)}, f32[2,8192]{1,0:T(2,128)}, u32[]{:S(2)}) copy-start(f32[2,8192]{1,0:T(2,128)} %param.15) | copy-start | bytes 196612
  2.9 22.3 %copy-start.4 = (bf16[768,256]{1,0:T(8,128)(2,1)S(1)}, bf16[768,256]{1,0:T(8,128)(2,1)}, u32[]{:S(2)}) copy-start(bf16[768,256]{1,0:T(8,128)(2,1)} %constant.20.clone.te_ref) | copy-start | bytes 1179652
  3.0 22.3 %copy-start.6 = (bf16[768,256]{1,0:T(8,128)(2,1)S(1)}, bf16[768,256]{1,0:T(8,128)(2,1)}, u32[]{:S(2)}) copy-start(bf16[768,256]{1,0:T(8,128)(2,1)} %constant.21.clone.to_ref) | copy-start | bytes 1179652
  3.0 22.3 %copy-start.9 = (bf16[256,384]{1,0:T(8,128)(2,1)S(1)}, bf16[256,384]{1,0:T(8,128)(2,1)}, u32[]{:S(2)}) copy-start(bf16[256,384]{1,0:T(8,128)(2,1)} %constant.18.clone.wf_ref) | copy-start | bytes 589828
  3.0 27.0 %all-to-all-start = ((f32[64,16,128]{2,1,0:T(8,128)}), f32[64,16,128]{2,1,0:T(8,128)S(1)}, u32[]{:S(2)}, u32[]{:S(2)}) async-start(f32[64,16,128]{2,1,0:T(8,128)} %bitcast.30), calls=%async_computation | async-start | bytes 1048576 | tf_op jit(solution)/shard_map/all_to_all | solution.py:306
  17.3 7.9 %copy-start.7 = (f32[2,128,256]{2,1,0:T(8,128)S(1)}, f32[2,128,256]{2,1,0:T(8,128)}, u32[]{:S(2)}) copy-start(f32[2,128,256]{2,1,0:T(8,128)} %constant.19.clone.tw_ref) | copy-start | bytes 786436
  17.3 6.4 %collective-permute-start = (f32[128,128]{1,0:T(8,128)S(1)}, f32[128,128]{1,0:T(8,128)S(1)}, u32[]{:S(2)}, u32[]{:S(2)}) collective-permute-start(f32[128,128]{1,0:T(8,128)S(1)} %bitcast.31), channel_id=1, source_target_pairs={{0,128},{64,192},{128,0},{192,64},{1,129},{65,193},{129,1},{193,65... | collective-permute-start | bytes 196616 | tf_op jit(solution)/shard_map/ppermute | solution.py:303
  23.8 1.4 %collective-permute-start.1 = (f32[256,128]{1,0:T(8,128)S(1)}, f32[256,128]{1,0:T(8,128)S(1)}, u32[]{:S(2)}, u32[]{:S(2)}) collective-permute-start(f32[256,128]{1,0:T(8,128)S(1)} %pad_maximum_fusion.near_ref), channel_id=1, source_target_pairs={{0,64},{64,0},{128,192},{192,128},{1,65},{65,1},{129,193},{193,129... | collective-permute-start | bytes 393224 | tf_op jit(solution)/shard_map/ppermute | solution.py:303
  23.9 6.1 %copy-start.5 = (bf16[768,256]{1,0:T(8,128)(2,1)S(1)}, bf16[768,256]{1,0:T(8,128)(2,1)}, u32[]{:S(2)}) copy-start(bf16[768,256]{1,0:T(8,128)(2,1)} %constant.23.clone.tb_ref) | copy-start | bytes 1179652
  23.9 6.1 %copy-start.8 = (bf16[128,768]{1,0:T(8,128)(2,1)S(1)}, bf16[128,768]{1,0:T(8,128)(2,1)}, u32[]{:S(2)}) copy-start(bf16[128,768]{1,0:T(8,128)(2,1)} %constant.22.clone.wi_ref) | copy-start | bytes 589828
  32.7 10.9 %copy-start.10 = (f32[2,256,256]{2,1,0:T(8,128)S(1)}, f32[2,256,256]{2,1,0:T(8,128)}, u32[]{:S(2)}) copy-start(f32[2,256,256]{2,1,0:T(8,128)} %get-tuple-element.13.cross_ref) | copy-start | bytes 1572868
  32.8 22.9 %all-to-all-start.1 = ((f32[64,16,128]{2,1,0:T(8,128)}), f32[64,16,128]{2,1,0:T(8,128)S(1)}, u32[]{:S(2)}, u32[]{:S(2)}) async-start(f32[64,16,128]{2,1,0:T(8,128)} %get-tuple-element.12), calls=%async_computation.1 | async-start | bytes 1048576 | tf_op jit(solution)/shard_map/all_to_all | solution.py:306
  43.7 12.0 %copy-start.2 = (f32[1,512,128]{2,1,0:T(8,128)S(1)}, f32[1,512,128]{2,1,0:T(8,128)}, u32[]{:S(2)}) copy-start(f32[1,512,128]{2,1,0:T(8,128)} %param.13) | copy-start | bytes 786436
  43.7 11.9 %copy-start.3 = (f32[1,512,128]{2,1,0:T(8,128)S(1)}, f32[1,512,128]{2,1,0:T(8,128)}, u32[]{:S(2)}) copy-start(f32[1,512,128]{2,1,0:T(8,128)} %param.14) | copy-start | bytes 786436
  45.0 1.4 %collective-permute-start.2 = (f32[256,128]{1,0:T(8,128)S(1)}, f32[256,128]{1,0:T(8,128)S(1)}, u32[]{:S(2)}, u32[]{:S(2)}) collective-permute-start(f32[256,128]{1,0:T(8,128)S(1)} %get-tuple-element.15), channel_id=1, source_target_pairs={{0,64},{64,0},{128,192},{192,128},{1,65},{65,1},{129,193},{193,129... | collective-permute-start | bytes 393224 | tf_op jit(solution)/shard_map/ppermute | solution.py:303
  46.4 9.2 %copy-start = (f32[1,512,128]{2,1,0:T(8,128)S(1)}, f32[1,512,128]{2,1,0:T(8,128)}, u32[]{:S(2)}) copy-start(f32[1,512,128]{2,1,0:T(8,128)} %param.11) | copy-start | bytes 786436
  46.4 9.2 %copy-start.1 = (f32[1,512,128]{2,1,0:T(8,128)S(1)}, f32[1,512,128]{2,1,0:T(8,128)}, u32[]{:S(2)}) copy-start(f32[1,512,128]{2,1,0:T(8,128)} %param.12) | copy-start | bytes 786436
  46.5 7.0 %collective-permute-start.3 = (f32[128,128]{1,0:T(8,128)S(1)}, f32[128,128]{1,0:T(8,128)S(1)}, u32[]{:S(2)}, u32[]{:S(2)}) collective-permute-start(f32[128,128]{1,0:T(8,128)S(1)} %get-tuple-element.20), channel_id=1, source_target_pairs={{0,128},{64,192},{128,0},{192,64},{1,129},{65,193},{129,1},{193,65... | collective-permute-start | bytes 196616 | tf_op jit(solution)/shard_map/ppermute | solution.py:303

commit v4 on v3

--- a/solution.py
+++ b/solution.py
@@ -9,7 +9,7 @@
 TOK = 64
 SEQ = 4
 FIRST_OUT = 42
-FIRST_HOME = 42
+FIRST_HOME = 40
 ROWS = 512
 WIDTH = 128
 LENGTH = TOK * ROWS

time: 57.2 us -> 57.9 us (1.012)
  starting transfers between devices: 27.2 us -> 28.1 us
    all_to_all x2, starting transfers between devices: 25.3 us -> 26.1 us  [exchange(): lax.all_to_all(block.reshape(TOK, 16, 128), 'tok', split_axis=0, concat_a...]
where the time goes in v4:
time: 57.9 us; the launch traced here: 57.6 us
  starting transfers between devices  28.1 us (49%)
  waiting for transfers between devices  19.5 us (34%)
  Pallas kernels  9.04 us (16%)
  between operations  0.84 us (1%)
    all_to_all x2, starting transfers between devices, exchange(): lax.all_to_all(block.reshape(TOK, 16, 128), 'tok', split_axis=0, concat_a...  26.1 us
    ppermute x4, waiting for transfers between devices, swap(): return lax.ppermute(block, 'seq', [(s, s ^ k) for s in range(SEQ)])  14.2 us
    all_to_all x2, waiting for transfers between devices, exchange(): lax.all_to_all(block.reshape(TOK, 16, 128), 'tok', split_axis=0, concat_a...  5.25 us
    pallas_call x1, Pallas kernels, body(): pl.pallas_call(spectral_kernel, out_shape=(shape(TOK, 16, 128), pltpu.HBM...  2.74 us
    pallas_call x1, Pallas kernels, body(): pl.pallas_call(send_kernel, out_shape=shape(TOK * 2, 8, 128), in_specs=[H...  2.29 us
    ppermute x4, starting transfers between devices, swap(): return lax.ppermute(block, 'seq', [(s, s ^ k) for s in range(SEQ)])  1.96 us
    pallas_call x1, Pallas kernels, body(): pl.pallas_call(taps_kernel, out_shape=shape(2, 2 * OUTER, INNER), in_spec...  1.64 us
    pallas_call x1, Pallas kernels, body(): pl.pallas_call(terms_kernel, out_shape=(shape(256, 128),) * 2, in_specs=[...  1.26 us
  transfers between devices with their start and end apart: 6, of which 6 were waited for; matrix products, arithmetic and copies ran while one was open for 0% of the time, Pallas kernels for 5%

profile of v4, /device:TPU:4, one launch (start us, length us, event | category | flops | bytes accessed | tf_op | source)
XLA Modules:
  0.0 57.6 jit_solution(3084933695156881300)
XLA Ops:
  0.6 2.3 %send.1 = f32[128,8,128]{2,1,0:T(8,128)} custom-call(f32[512,128]{1,0:T(8,128)} %bitcast.21, f32[512,128]{1,0:T(8,128)} %bitcast.23, f32[512,128]{1,0:T(8,128)} %bitcast.25, f32[512,128]{1,0:T(8,128)} %bitcast.27), custom_call_target="tpu_custom_call" | custom-call | tf_op jit(solution)/shard_map/send/pallas_call | solution.py:319
  2.9 0.0 copy-start.11
  2.9 0.0 copy-start.4
  3.0 0.0 copy-start.6
  3.0 0.0 copy-start.9
  3.0 14.3 %all-to-all-start = ((f32[64,16,128]{2,1,0:T(8,128)}), f32[64,16,128]{2,1,0:T(8,128)S(1)}, u32[]{:S(2)}, u32[]{:S(2)}) async-start(f32[64,16,128]{2,1,0:T(8,128)} %bitcast.30), calls=%async_computation | async-start | bytes 1048576 | tf_op jit(solution)/shard_map/all_to_all | solution.py:306
  17.3 0.0 copy-start.7
  17.3 0.0 copy-done.11
  17.3 0.9 %collective-permute-start = (f32[128,128]{1,0:T(8,128)S(1)}, f32[128,128]{1,0:T(8,128)S(1)}, u32[]{:S(2)}, u32[]{:S(2)}) collective-permute-start(f32[128,128]{1,0:T(8,128)S(1)} %bitcast.31), channel_id=1, source_target_pairs={{0,128},{64,192},{128,0},{192,64},{1,129},{65,193},{129,1},{193,65... | collective-permute-start | bytes 196616 | tf_op jit(solution)/shard_map/ppermute | solution.py:303
  18.2 5.5 %collective-permute-done = f32[128,128]{1,0:T(8,128)S(1)} collective-permute-done((f32[128,128]{1,0:T(8,128)S(1)}, f32[128,128]{1,0:T(8,128)S(1)}, u32[]{:S(2)}, u32[]{:S(2)}) %collective-permute-start) | collective-permute-done | bytes 65568 | tf_op jit(solution)/shard_map/ppermute | solution.py:303
  23.8 0.1 collective-permute-start.1
  23.9 0.0 copy-start.5
  23.9 0.0 copy-start.8
  23.9 1.3 %collective-permute-done.1.far_ref = f32[256,128]{1,0:T(8,128)S(1)} collective-permute-done((f32[256,128]{1,0:T(8,128)S(1)}, f32[256,128]{1,0:T(8,128)S(1)}, u32[]{:S(2)}, u32[]{:S(2)}) %collective-permute-start.1) | collective-permute-done | bytes 131104 | tf_op jit(solution)/shard_map/ppermute | solution.py:303
  25.2 0.0 copy-done.4
  25.2 0.0 copy-done.6
  25.2 0.0 copy-done.9
  25.2 0.0 copy-done.7
  25.2 1.6 %taps.1.taps_ref = f32[2,256,256]{2,1,0:T(8,128)S(1)} custom-call(s32[4]{0:T(128)S(1)} %iota_xor_fusion.part_ref, f32[256,128]{1,0:T(8,128)S(1)} %pad_maximum_fusion.near_ref, f32[256,128]{1,0:T(8,128)S(1)} %collective-permute-done.1.far_ref, bf16[256,384]{1,0:T(8,128)(2,1)S(1)} %copy-done.9, f32[2,128,256]{2,1,0:T(8,128)S(1)} %copy-done.7, ...), custom_call_target="tpu_custom_call" | custom-call | flops 800000000 | bytes 1000000 | tf_op jit(solution)/shard_map/taps/pallas_call | solution.py:330
  26.9 3.1 %all-to-all-done = f32[64,16,128]{2,1,0:T(8,128)S(1)} async-done(((f32[64,16,128]{2,1,0:T(8,128)}), f32[64,16,128]{2,1,0:T(8,128)S(1)}, u32[]{:S(2)}, u32[]{:S(2)}) %all-to-all-start) | async-done | bytes 524320 | tf_op jit(solution)/shard_map/all_to_all | solution.py:306
  30.0 0.0 copy-done.5
  30.0 0.0 copy-done.8
  30.0 2.7 %spectral.1 = (f32[64,16,128]{2,1,0:T(8,128)}, f32[2,256,256]{2,1,0:T(8,128)}) custom-call(f32[1024,128]{1,0:T(8,128)S(1)} %bitcast.29, f32[2,256,256]{2,1,0:T(8,128)S(1)} %taps.1.taps_ref, bf16[256,384]{1,0:T(8,128)(2,1)S(1)} %copy-done.9, bf16[128,768]{1,0:T(8,128)(2,1)S(1)} %copy-done.8, f32[2,128,256]{2,1,0:T(8,128)S(1)} %copy-done.7, ...), custom_call_target="tpu_custom_call" | custom-call | flops 3200000000 | bytes 4000000 | tf_op jit(solution)/shard_map/spectral/pallas_call | solution.py:342
  32.7 0.0 copy-start.10
  32.8 11.8 %all-to-all-start.1 = ((f32[64,16,128]{2,1,0:T(8,128)}), f32[64,16,128]{2,1,0:T(8,128)S(1)}, u32[]{:S(2)}, u32[]{:S(2)}) async-start(f32[64,16,128]{2,1,0:T(8,128)} %get-tuple-element.12), calls=%async_computation.1 | async-start | bytes 1048576 | tf_op jit(solution)/shard_map/all_to_all | solution.py:306
  44.6 0.0 copy-done.10
  44.6 0.0 copy-start.2
  44.6 0.0 copy-start.3
  44.6 1.3 %terms.1 = (f32[256,128]{1,0:T(8,128)S(1)}, f32[256,128]{1,0:T(8,128)S(1)}) custom-call(s32[4]{0:T(128)S(1)} %iota_xor_fusion.part_ref, f32[2,256,256]{2,1,0:T(8,128)S(1)} %copy-done.10, bf16[128,768]{1,0:T(8,128)(2,1)S(1)} %copy-done.8, f32[2,128,256]{2,1,0:T(8,128)S(1)} %copy-done.7, bf16[768,256]{1,0:T(8,128)(2,1)S(1)} %copy-done.4, ...), custom_call_target="tpu_custom_call" | custom-call | flops 800000000 | bytes 1000000 | tf_op jit(solution)/shard_map/terms/pallas_call | solution.py:356
  45.9 0.1 collective-permute-start.2
  46.0 1.3 %collective-permute-done.2 = f32[256,128]{1,0:T(8,128)S(1)} collective-permute-done((f32[256,128]{1,0:T(8,128)S(1)}, f32[256,128]{1,0:T(8,128)S(1)}, u32[]{:S(2)}, u32[]{:S(2)}) %collective-permute-start.2) | collective-permute-done | bytes 131104 | tf_op jit(solution)/shard_map/ppermute | solution.py:303
  47.3 0.0 copy-start
  47.3 0.0 copy-start.1
  47.3 0.9 %collective-permute-start.3 = (f32[128,128]{1,0:T(8,128)S(1)}, f32[128,128]{1,0:T(8,128)S(1)}, u32[]{:S(2)}, u32[]{:S(2)}) collective-permute-start(f32[128,128]{1,0:T(8,128)S(1)} %get-tuple-element.20), channel_id=1, source_target_pairs={{0,128},{64,192},{128,0},{192,64},{1,129},{65,193},{129,1},{193,65... | collective-permute-start | bytes 196616 | tf_op jit(solution)/shard_map/ppermute | solution.py:303
  48.2 6.0 %collective-permute-done.3.far_ref = f32[128,128]{1,0:T(8,128)S(1)} collective-permute-done((f32[128,128]{1,0:T(8,128)S(1)}, f32[128,128]{1,0:T(8,128)S(1)}, u32[]{:S(2)}, u32[]{:S(2)}) %collective-permute-start.3) | collective-permute-done | bytes 65568 | tf_op jit(solution)/shard_map/ppermute | solution.py:303
  54.3 2.1 %all-to-all-done.1 = f32[64,16,128]{2,1,0:T(8,128)S(1)} async-done(((f32[64,16,128]{2,1,0:T(8,128)}), f32[64,16,128]{2,1,0:T(8,128)S(1)}, u32[]{:S(2)}, u32[]{:S(2)}) %all-to-all-start.1) | async-done | bytes 524320 | tf_op jit(solution)/shard_map/all_to_all | solution.py:306
  56.4 0.0 copy-done.2
  56.4 0.0 copy-done.3
  56.4 0.0 copy-done
  56.4 0.0 copy-done.1
  56.4 1.1 %finish.1 = (f32[512,128]{1,0:T(8,128)}, f32[512,128]{1,0:T(8,128)}, f32[512,128]{1,0:T(8,128)}, f32[128,128]{1,0:T(8,128)}) custom-call(f32[1024,128]{1,0:T(8,128)S(1)} %bitcast.20, f32[512,128]{1,0:T(8,128)S(1)} %bitcast.22, f32[512,128]{1,0:T(8,128)S(1)} %bitcast.24, f32[512,128]{1,0:T(8,128)S(1)} %bitcast.26, f32[512,128]{1,0:T(8,128)S(1)} %bitcast.28, ...), custom_call_target="tpu_custom_call" | custom-call | tf_op jit(solution)/shard_map/finish/pallas_call | solution.py:370
  (4 shorter events, 0.0 us)
Async XLA Ops:
  2.9 14.4 %copy-start.11 = (f32[2,8192]{1,0:T(2,128)S(1)}, f32[2,8192]{1,0:T(2,128)}, u32[]{:S(2)}) copy-start(f32[2,8192]{1,0:T(2,128)} %param.15) | copy-start | bytes 196612
  2.9 22.3 %copy-start.4 = (bf16[768,256]{1,0:T(8,128)(2,1)S(1)}, bf16[768,256]{1,0:T(8,128)(2,1)}, u32[]{:S(2)}) copy-start(bf16[768,256]{1,0:T(8,128)(2,1)} %constant.20.clone.te_ref) | copy-start | bytes 1179652
  3.0 22.3 %copy-start.6 = (bf16[768,256]{1,0:T(8,128)(2,1)S(1)}, bf16[768,256]{1,0:T(8,128)(2,1)}, u32[]{:S(2)}) copy-start(bf16[768,256]{1,0:T(8,128)(2,1)} %constant.21.clone.to_ref) | copy-start | bytes 1179652
  3.0 22.3 %copy-start.9 = (bf16[256,384]{1,0:T(8,128)(2,1)S(1)}, bf16[256,384]{1,0:T(8,128)(2,1)}, u32[]{:S(2)}) copy-start(bf16[256,384]{1,0:T(8,128)(2,1)} %constant.18.clone.wf_ref) | copy-start | bytes 589828
  3.0 27.0 %all-to-all-start = ((f32[64,16,128]{2,1,0:T(8,128)}), f32[64,16,128]{2,1,0:T(8,128)S(1)}, u32[]{:S(2)}, u32[]{:S(2)}) async-start(f32[64,16,128]{2,1,0:T(8,128)} %bitcast.30), calls=%async_computation | async-start | bytes 1048576 | tf_op jit(solution)/shard_map/all_to_all | solution.py:306
  17.3 7.9 %copy-start.7 = (f32[2,128,256]{2,1,0:T(8,128)S(1)}, f32[2,128,256]{2,1,0:T(8,128)}, u32[]{:S(2)}) copy-start(f32[2,128,256]{2,1,0:T(8,128)} %constant.19.clone.tw_ref) | copy-start | bytes 786436
  17.3 6.4 %collective-permute-start = (f32[128,128]{1,0:T(8,128)S(1)}, f32[128,128]{1,0:T(8,128)S(1)}, u32[]{:S(2)}, u32[]{:S(2)}) collective-permute-start(f32[128,128]{1,0:T(8,128)S(1)} %bitcast.31), channel_id=1, source_target_pairs={{0,128},{64,192},{128,0},{192,64},{1,129},{65,193},{129,1},{193,65... | collective-permute-start | bytes 196616 | tf_op jit(solution)/shard_map/ppermute | solution.py:303
  23.8 1.4 %collective-permute-start.1 = (f32[256,128]{1,0:T(8,128)S(1)}, f32[256,128]{1,0:T(8,128)S(1)}, u32[]{:S(2)}, u32[]{:S(2)}) collective-permute-start(f32[256,128]{1,0:T(8,128)S(1)} %pad_maximum_fusion.near_ref), channel_id=1, source_target_pairs={{0,64},{64,0},{128,192},{192,128},{1,65},{65,1},{129,193},{193,129... | collective-permute-start | bytes 393224 | tf_op jit(solution)/shard_map/ppermute | solution.py:303
  23.9 6.1 %copy-start.5 = (bf16[768,256]{1,0:T(8,128)(2,1)S(1)}, bf16[768,256]{1,0:T(8,128)(2,1)}, u32[]{:S(2)}) copy-start(bf16[768,256]{1,0:T(8,128)(2,1)} %constant.23.clone.tb_ref) | copy-start | bytes 1179652
  23.9 6.1 %copy-start.8 = (bf16[128,768]{1,0:T(8,128)(2,1)S(1)}, bf16[128,768]{1,0:T(8,128)(2,1)}, u32[]{:S(2)}) copy-start(bf16[128,768]{1,0:T(8,128)(2,1)} %constant.22.clone.wi_ref) | copy-start | bytes 589828
  32.7 11.8 %copy-start.10 = (f32[2,256,256]{2,1,0:T(8,128)S(1)}, f32[2,256,256]{2,1,0:T(8,128)}, u32[]{:S(2)}) copy-start(f32[2,256,256]{2,1,0:T(8,128)} %get-tuple-element.13.cross_ref) | copy-start | bytes 1572868
  32.8 23.7 %all-to-all-start.1 = ((f32[64,16,128]{2,1,0:T(8,128)}), f32[64,16,128]{2,1,0:T(8,128)S(1)}, u32[]{:S(2)}, u32[]{:S(2)}) async-start(f32[64,16,128]{2,1,0:T(8,128)} %get-tuple-element.12), calls=%async_computation.1 | async-start | bytes 1048576 | tf_op jit(solution)/shard_map/all_to_all | solution.py:306
  44.6 11.9 %copy-start.2 = (f32[1,512,128]{2,1,0:T(8,128)S(1)}, f32[1,512,128]{2,1,0:T(8,128)}, u32[]{:S(2)}) copy-start(f32[1,512,128]{2,1,0:T(8,128)} %param.13) | copy-start | bytes 786436
  44.6 11.8 %copy-start.3 = (f32[1,512,128]{2,1,0:T(8,128)S(1)}, f32[1,512,128]{2,1,0:T(8,128)}, u32[]{:S(2)}) copy-start(f32[1,512,128]{2,1,0:T(8,128)} %param.14) | copy-start | bytes 786436
  45.9 1.4 %collective-permute-start.2 = (f32[256,128]{1,0:T(8,128)S(1)}, f32[256,128]{1,0:T(8,128)S(1)}, u32[]{:S(2)}, u32[]{:S(2)}) collective-permute-start(f32[256,128]{1,0:T(8,128)S(1)} %get-tuple-element.15), channel_id=1, source_target_pairs={{0,64},{64,0},{128,192},{192,128},{1,65},{65,1},{129,193},{193,129... | collective-permute-start | bytes 393224 | tf_op jit(solution)/shard_map/ppermute | solution.py:303
  47.3 9.1 %copy-start = (f32[1,512,128]{2,1,0:T(8,128)S(1)}, f32[1,512,128]{2,1,0:T(8,128)}, u32[]{:S(2)}) copy-start(f32[1,512,128]{2,1,0:T(8,128)} %param.11) | copy-start | bytes 786436
  47.3 9.1 %copy-start.1 = (f32[1,512,128]{2,1,0:T(8,128)S(1)}, f32[1,512,128]{2,1,0:T(8,128)}, u32[]{:S(2)}) copy-start(f32[1,512,128]{2,1,0:T(8,128)} %param.12) | copy-start | bytes 786436
  47.3 6.9 %collective-permute-start.3 = (f32[128,128]{1,0:T(8,128)S(1)}, f32[128,128]{1,0:T(8,128)S(1)}, u32[]{:S(2)}, u32[]{:S(2)}) collective-permute-start(f32[128,128]{1,0:T(8,128)S(1)} %get-tuple-element.20), channel_id=1, source_target_pairs={{0,128},{64,192},{128,0},{192,64},{1,129},{65,193},{129,1},{193,65... | collective-permute-start | bytes 196616 | tf_op jit(solution)/shard_map/ppermute | solution.py:303
